TPU v7x, 512 devices: a whole 4x8x8 slice. The times are simulated.
512 devices in a mesh: lev: 16 (over z_lo, y), lon: 32 (over x, z_hi, core).
Axes of the slice: x: 4, y: 8, z: 8 (z_hi: 4, z_lo: 2; z = z_hi * 2 + z_lo), core: 2. Of those that a mesh axis runs over, the one named last changes fastest.
Arguments:
- snapshot: bfloat16 [384, 48, 4096], P('lev', None, 'lon'), may hold values from -6 to 6
- cotangent: bfloat16 [384, 48, 4096], P(None, 'lev', 'lon'), may hold values from -6 to 6
- ocean_mask: int32 [48, 4096], P('lev', 'lon'), may hold values 0 or 1
- kernel: bfloat16 [384, 49], replicated, may hold values from -0.875 to 0.875
- norm_gain: float32 [384], replicated, may hold values from 0.1 to 1.9
- norm_shift: float32 [384], replicated, may hold values from -3 to 3
- weight_in: bfloat16 [384, 1536], replicated, may hold values from -0.3125 to 0.3125
- weight_out: bfloat16 [1536, 384], replicated, may hold values from -0.15625 to 0.15625
Outputs:
- result: bfloat16 [384, 48, 4096], P(None, 'lev', 'lon')
- d_snapshot: bfloat16 [384, 48, 4096], P('lev', None, 'lon')
- kernel_grad: float32 [384, 49], replicated
All inputs are finite; a program needn't handle non-finite values. No bound on the sum of `ocean_mask` on one device may be relied on, other than what follows from the above.
Results may differ from a plain program's by a relative error of at most 0.0057.
Values may be sent and summed in bfloat16 or wider, within the bound.
A program may use at most 64 MiB of HBM per device.

v0:
```python
import jax
import jax.numpy as jnp
from jax import lax
from jax.sharding import PartitionSpec as P

TAPS = 7


epsilon = 1e-06
root_half = 0.7071067811865476
inv_root_tau = 0.3989422804014327


def padded_2(shard, sides, width):
    for axis, dim in sides:
        count, length = (lax.axis_size(axis), shard.shape[dim])
        up = [(i, (i + 1) % count) for i in range(count)]
        down = [(j, i) for i, j in up]
        last = lax.slice_in_dim(shard, length - width, length, axis=dim)
        leading = lax.slice_in_dim(shard, 0, width, axis=dim)
        before = lax.ppermute(last, axis, up)
        after = lax.ppermute(leading, axis, down)
        shard = jnp.concatenate([before, shard, after], axis=dim)
    return shard


def taps(padded, weights, height, width):
    source = padded.astype(jnp.float32)
    total = jnp.zeros((padded.shape[0], height, width), jnp.float32)
    for row_off in range(TAPS):
        for col_off in range(TAPS):
            piece = source[:, row_off : row_off + height, col_off : col_off + width]
            total = total + weights[:, row_off, col_off][:, None, None] * piece
    return total


def kernel_terms(padded, d_conv, height, width):
    source = padded.astype(jnp.float32)
    flat = d_conv.astype(jnp.float32)
    terms = []
    for row_off in range(TAPS):
        for col_off in range(TAPS):
            piece = source[:, row_off : row_off + height, col_off : col_off + width]
            terms.append(jnp.sum(flat * piece, axis=(1, 2)))
    return jnp.stack(terms, axis=1)


def fold_term(fold_rows, weights, width):
    reach = TAPS // 2
    lines = []
    for depth in range(reach):
        total = jnp.zeros((fold_rows.shape[0], width), jnp.float32)
        for source in range(reach - depth):
            for col_off in range(TAPS):
                piece = fold_rows[:, source, col_off : col_off + width].astype(jnp.float32)
                total = total + weights[:, reach + 1 + depth + source, col_off][:, None] * piece
        lines.append(total)
    return jnp.stack(lines[::-1], axis=1)


def gelu_slope(hidden):
    return (
        0.5 * (1.0 + lax.erf(hidden * root_half))
        + hidden * jnp.exp(-0.5 * hidden * hidden) * inv_root_tau
    )


def cell_pass(convolved, residual, incoming, ocean, norm_gain, norm_shift, weight_in, weight_out):
    centre = jnp.mean(convolved, axis=0, keepdims=True)
    centred = convolved - centre
    spread = jnp.mean(centred * centred, axis=0, keepdims=True)
    rstd = lax.rsqrt(spread + epsilon)
    normed = centred * rstd
    lifted = (normed * norm_gain[:, None] + norm_shift[:, None]).astype(jnp.bfloat16)
    hidden = lax.dot_general(
        weight_in, lifted, (((0,), (0,)), ((), ())), preferred_element_type=jnp.float32
    )
    active = jax.nn.gelu(hidden, approximate=False).astype(jnp.bfloat16)
    projected = lax.dot_general(
        weight_out, active, (((0,), (0,)), ((), ())), preferred_element_type=jnp.float32
    )
    wet = ocean.astype(jnp.float32)[None, :]
    result = (wet * (residual.astype(jnp.float32) + projected)).astype(jnp.bfloat16)
    upstream = incoming.astype(jnp.float32) * wet
    d_active = jnp.dot(
        weight_out, upstream.astype(jnp.bfloat16), preferred_element_type=jnp.float32
    )
    d_hidden = (d_active * gelu_slope(hidden)).astype(jnp.bfloat16)
    d_lifted = jnp.dot(weight_in, d_hidden, preferred_element_type=jnp.float32)
    d_normed = d_lifted * norm_gain[:, None]
    first = jnp.mean(d_normed, axis=0, keepdims=True)
    second = jnp.mean(d_normed * normed, axis=0, keepdims=True)
    d_conv = (rstd * (d_normed - first - normed * second)).astype(jnp.bfloat16)
    return (result, upstream, d_conv)


def fold_edge(edge_rows):
    lanes = lax.axis_size("lon")
    depth_rows = edge_rows.shape[1]
    span = edge_rows.shape[2]
    channels = edge_rows.shape[0]
    blocks = edge_rows.reshape(lanes, channels // lanes, depth_rows, span)
    spread = lax.all_to_all(blocks, "lon", split_axis=0, concat_axis=0, tiled=True)
    collected = lax.all_to_all(spread[::-1], "lon", split_axis=0, concat_axis=0, tiled=True)
    edge_rows = collected.reshape(channels, depth_rows, span)
    return edge_rows[:, ::-1, ::-1]


def tile_pad(tile):
    reach = TAPS // 2
    height = tile.shape[1]
    padded = padded_2(tile, (("lev", 1), ("lon", 2)), reach)
    position = lax.axis_index("lev")
    folded = fold_edge(padded[:, height : height + reach, :])
    lower = jnp.where(position == 0, jnp.zeros_like(padded[:, :reach]), padded[:, :reach])
    upper = jnp.where(
        position == lax.axis_size("lev") - 1, jnp.zeros_like(folded), padded[:, height + reach :]
    )
    regular = jnp.concatenate([lower, padded[:, reach : height + reach], upper], axis=1)
    return (regular, folded)


def shards(snapshot, cotangent, ocean_mask, kernel, norm_gain, norm_shift, weight_in, weight_out):
    reach = TAPS // 2
    levels = lax.axis_size("lev")
    channels = snapshot.shape[0] * levels
    height = snapshot.shape[1] // levels
    width = snapshot.shape[2]
    is_top = lax.axis_index("lev") == levels - 1
    weights = kernel.astype(jnp.float32).reshape(channels, TAPS, TAPS)
    tile = lax.all_to_all(snapshot, "lev", split_axis=1, concat_axis=0, tiled=True)
    regular, folded = tile_pad(tile)
    upper = jnp.where(is_top, folded, regular[:, height + reach :])
    padded = jnp.concatenate([regular[:, : height + reach], upper], axis=1)
    count = height * width
    convolved = taps(padded, weights, height, width)
    residual = padded[:, reach : height + reach, reach : width + reach]
    result, upstream, d_conv = cell_pass(
        convolved.reshape(channels, count),
        residual.reshape(channels, count),
        cotangent.reshape(channels, count),
        ocean_mask.reshape(count),
        norm_gain,
        norm_shift,
        weight_in,
        weight_out,
    )
    d_conv = d_conv.reshape(channels, height, width)
    local_terms = kernel_terms(padded, d_conv, height, width)
    kernel_grad = lax.psum(local_terms, ("lev", "lon"))
    d_regular, d_folded = tile_pad(d_conv)
    adjoint = taps(d_regular, weights[:, ::-1, ::-1], height, width)
    edge = jnp.where(is_top, fold_term(d_folded, weights, width), 0.0)
    adjoint = adjoint.at[:, height - reach :, :].add(edge)
    d_tile = (upstream.reshape(channels, height, width) + adjoint).astype(jnp.bfloat16)
    d_snapshot = lax.all_to_all(d_tile, "lev", split_axis=0, concat_axis=1, tiled=True)
    return (result.reshape(channels, height, width), d_snapshot, kernel_grad)


def solution(mesh):
    placed = (
        P("lev", None, "lon"),
        P(None, "lev", "lon"),
        P("lev", "lon"),
        P(),
        P(),
        P(),
        P(),
        P(),
    )
    return jax.shard_map(
        shards,
        mesh=mesh,
        in_specs=placed,
        out_specs=(P(None, "lev", "lon"), P("lev", None, "lon"), P()),
        check_vma=False,
    )
```

profile of v0, /device:TPU:1, one launch (start us, length us, event | category | flops | bytes accessed | tf_op | source)
XLA Modules:
  0.0 534.0 jit_solution(10195537101676007353)
XLA Ops:
  8.3 18.7 %all_to_all.56 = bf16[24,48,128]{2,0,1:T(8,128)(2,1)S(1)} all-to-all(bf16[24,48,128]{2,0,1:T(8,128)(2,1)S(1)} %copy.71), channel_id=1, replica_groups=mesh['lev'=16,'lon'=32] {'lev'}, dimensions={1} | all-to-all | bytes 589824 | tf_op jit(solution)/shard_map/all_to_all | solution.py:131
  27.0 4.6 collective-permute-start.1
  31.6 1.9 collective-permute-start
  33.5 3.1 collective-permute-done.1
  36.7 4.5 collective-permute-done
  43.3 9.5 %collective-permute-start.2 = (bf16[384,9,3]{0,2,1:T(4,128)(2,1)}, bf16[384,9,3]{0,2,1:T(4,128)(2,1)S(1)}, u32[]{:S(2)}, u32[]{:S(2)}) collective-permute-start(bf16[384,9,3]{0,2,1:T(4,128)(2,1)} %copy.74), channel_id=1, source_target_pairs={{0,1},{1,2},{2,3},{3,4},{4,5},{5,6},{6,7},{7,8},{8,9},{9,10},{10,1... | collective-permute-start | bytes 62216 | tf_op jit(solution)/shard_map/ppermute | solution.py:21
  53.2 1.9 collective-permute-start.3
  56.5 2.8 collective-permute-done.3
  60.6 2.5 pad_maximum_fusion
  64.3 2.1 copy.104
  66.3 3.0 reshape.525
  69.4 10.4 %all-to-all-start.1 = ((bf16[32,2,2412]{2,1,0:T(2,128)(2,1)}), bf16[32,2,2412]{2,1,0:T(2,128)(2,1)}, u32[]{:S(2)}, u32[]{:S(2)}) async-start(bf16[32,2,2412]{2,1,0:T(2,128)(2,1)} %reshape.525), calls=%async_computation.1 | async-start | bytes 622592 | tf_op jit(solution)/shard_map/all_to_all | solution.py:103
  83.1 11.3 %all-to-all-done.1 = bf16[32,2,2412]{2,1,0:T(2,128)(2,1)} async-done(((bf16[32,2,2412]{2,1,0:T(2,128)(2,1)}), bf16[32,2,2412]{2,1,0:T(2,128)(2,1)}, u32[]{:S(2)}, u32[]{:S(2)}) %all-to-all-start.1) | async-done | bytes 308768 | tf_op jit(solution)/shard_map/all_to_all | solution.py:103
  94.4 3.0 reshape.526
  97.3 2.1 reverse_bitcast_fusion.1
  99.4 3.1 reshape.527
  102.5 5.0 all-to-all-start.2
  109.1 1.9 copy.82
  111.1 1.9 slice_reduce_fusion.48
  116.8 5.2 all-to-all-done.2
  122.0 3.0 reshape.528
  124.9 2.1 copy.79
  127.0 2.1 reshape.466
  129.2 9.6 %reverse.70 = bf16[384,3,256]{2,0,1:T(8,128)(2,1)} reverse(bf16[384,3,256]{2,0,1:T(8,128)(2,1)} %bitcast.112), dimensions={1,2} | reverse | bytes 1179648
  141.3 10.8 %fusion.209 = (f32[3,128]{1,0:T(4,128)S(1)}, f32[384,3,128]{2,0,1:T(8,128)S(1)}) fusion(f32[384,9,134]{2,0,1:T(8,128)S(1)} %maximum_convert_fusion, f32[384]{0:T(512)S(1)} %get-tuple-element.88, f32[384]{0:T(512)S(1)} %get-tuple-element.89, f32[384]{0:T(512)S(1)} %get-tuple-element.90, f32[384]{0:T(512)S(1)} %get-tuple-element.91, f32[384]{0:T(512)S(1)} %copy-done.21, ...), kind=kLoop, calls=%fused_computation.427 | loop fusion | flops 14450304 | bytes 29568000 | tf_op jit(solution)/shard_map/reduce_sum | solution.py:69
  153.4 2.2 convolution_bitcast_fusion.1
  155.6 3.8 fusion.131
  160.1 1.9 collective-permute-start.5
  162.0 3.4 collective-permute-start.4
  165.4 4.7 collective-permute-done.5
  170.0 4.0 collective-permute-done.4
  176.2 3.0 collective-permute-start.6
  179.6 2.2 collective-permute-start.7
  182.3 3.6 collective-permute-done.7
  187.2 2.0 pad_maximum_fusion.1
  194.3 11.2 %all-to-all-start.3 = ((bf16[32,2,2412]{2,1,0:T(2,128)(2,1)}), bf16[32,2,2412]{2,1,0:T(2,128)(2,1)S(1)}, u32[]{:S(2)}, u32[]{:S(2)}) async-start(bf16[32,2,2412]{2,1,0:T(2,128)(2,1)} %reshape.529), calls=%async_computation.3 | async-start | bytes 622592 | tf_op jit(solution)/shard_map/all_to_all | solution.py:103
  206.8 13.0 %fusion.75 = (f32[384]{0:T(512)S(1)}, f32[384]{0:T(512)}, f32[384]{0:T(512)}, f32[384]{0:T(512)}, f32[384]{0:T(512)}, /*index=5*/f32[384]{0:T(512)}, f32[384]{0:...) fusion(bf16[384,3,128]{2,0,1:T(8,128)(2,1)S(1)} %copy.83, ...), kind=kLoop, calls=%fused_computation.142 | loop fusion | flops 5448960 | bytes 10939392 | tf_op jit(solution)/shard_map/reduce_sum | solution.py:44
  222.0 3.0 reshape.531
  225.0 9.6 %all-to-all-start.4 = ((bf16[32,2,2412]{2,1,0:T(2,128)(2,1)}), bf16[32,2,2412]{2,1,0:T(2,128)(2,1)S(1)}, u32[]{:S(2)}, u32[]{:S(2)}) async-start(bf16[32,2,2412]{2,1,0:T(2,128)(2,1)} %reshape.531), calls=%async_computation.4 | async-start | bytes 622592 | tf_op jit(solution)/shard_map/all_to_all | solution.py:104
  234.9 9.0 %fusion.73 = (f32[384]{0:T(512)S(1)}, f32[384]{0:T(512)S(1)}, f32[384]{0:T(512)S(1)}, f32[384]{0:T(512)S(1)}, f32[384]{0:T(512)S(1)}, /*index=5*/f32[384]{0:T(51...) fusion(bf16[384,3,128]{2,0,1:T(8,128)(2,1)S(1)} %copy.83, ...), kind=kLoop, calls=%fused_computation.140 | loop fusion | flops 3976320 | bytes 7982592 | tf_op jit(solution)/shard_map/reduce_sum | solution.py:44
  252.0 3.5 fusion.74
  256.1 7.0 %stack.206 = f32[384,49]{0,1:T(8,128)} concatenate(f32[384,1]{0,1:T(1,128)} %stack.157, f32[384,1]{0,1:T(1,128)S(1)} %stack.158, f32[384,1]{0,1:T(1,128)S(1)} %stack.159, f32[384,1]{0,1:T(1,128)S(1)} %stack.160, f32[384,1]{0,1:T(1,128)S(1)} %stack.161, f32[384,1]{0,1:T(1,128)S(1)} %stack.162, f32[384,1]{0,1:T(1,128)S(1)} %stack.163, f32[384,1]{0,1:T(1,128)S(1)} %stack.164, ...), dimensions={1} | concatenate | bytes 150528 | tf_op jit(solution)/shard_map/stack | solution.py:45
  263.2 2.2 maximum_convert_fusion.1
  285.9 11.7 %fusion.79 = bf16[384,3,128]{2,0,1:T(8,128)(2,1)S(1)} fusion(f32[384,9,134]{2,0,1:T(8,128)S(1)} %copy-done.3, f32[384,1,128]{2,0,1:T(8,128)S(1)} %fusion.154, f32[384,1,128]{2,0,1:T(8,128)S(1)} %fusion.140, f32[384,1,128]{2,0,1:T(8,128)S(1)} %fusion.160, f32[3,128]{1,0:T(4,128)} %get-tuple-element.168, f32[384]{0:T(512)S(1)} %copy-done.14, ...), kind=kLoop, calls=%fused_computation.148 | loop fusion | flops 15482880 | bytes 30157824 | tf_op jit(solution)/shard_map/convert_element_type | solution.py:155
  298.6 4.2 all-to-all-start.5
  302.8 7.5 %fusion.20 = bf16[384,384]{0,1:T(8,128)(2,1)} fusion(f32[384,384]{0,1:T(8,128)} %copy.81, bf16[1536,384]{1,0:T(8,128)(2,1)} %param.19, f32[1536,384]{0,1:T(8,128)S(1)} %copy-done.6, f32[384]{0:T(512)} %copy-done.93), kind=kOutput, calls=%fused_computation.86 | convolution fusion | flops 491765760 | bytes 4425216 | tf_op jit(solution)/shard_map/dot_general | solution.py:79
  312.1 2.6 all-to-all-done.5
  316.5 208.8 %all-reduce.2.cloned.1.call-done = f32[384,49]{0,1:T(8,128)} async-done(((f32[384,49]{0,1:T(8,128)}), f32[384,49]{0,1:T(8,128)}) %all-reduce.2.cloned.1.call-update) | async-done | bytes 75280 | tf_op jit(solution)/shard_map/psum | solution.py:150
  (355 shorter events, 67.1 us)
Async XLA Ops:
  7.2 146.2 %copy-start = (bf16[384,1536]{1,0:T(8,128)(2,1)S(1)}, bf16[384,1536]{1,0:T(8,128)(2,1)}, u32[]{:S(2)}) copy-start(bf16[384,1536]{1,0:T(8,128)(2,1)} %param.18) | copy-start | bytes 3538948
  27.0 9.7 %copy-start.4 = (bf16[24,48,128]{2,0,1:T(8,128)(2,1)}, bf16[24,48,128]{2,0,1:T(8,128)(2,1)S(1)}, u32[]{:S(2)}) copy-start(bf16[24,48,128]{2,0,1:T(8,128)(2,1)S(1)} %all_to_all.56) | copy-start | bytes 884740
  27.0 9.7 %collective-permute-start.1 = (bf16[384,3,128]{2,0,1:T(8,128)(2,1)S(1)}, bf16[384,3,128]{2,0,1:T(8,128)(2,1)S(1)}, u32[]{:S(2)}, u32[]{:S(2)}) collective-permute-start(bf16[384,3,128]{2,0,1:T(8,128)(2,1)S(1)} %bitcast.106), channel_id=1, source_target_pairs={{32,0},{64,32},{96,64},{128,96},{160,128},{192,160},{224,192},{256... | collective-permute-start | bytes 884744 | tf_op jit(solution)/shard_map/ppermute | solution.py:22
  31.6 9.6 %collective-permute-start = (bf16[384,3,128]{2,0,1:T(8,128)(2,1)S(1)}, bf16[384,3,128]{2,0,1:T(8,128)(2,1)S(1)}, u32[]{:S(2)}, u32[]{:S(2)}) collective-permute-start(bf16[384,3,128]{2,0,1:T(8,128)(2,1)S(1)} %bitcast.107), channel_id=1, source_target_pairs={{0,32},{32,64},{64,96},{96,128},{128,160},{160,192},{192,224},{224... | collective-permute-start | bytes 884744 | tf_op jit(solution)/shard_map/ppermute | solution.py:21
  43.3 11.8 %collective-permute-start.2 = (bf16[384,9,3]{0,2,1:T(4,128)(2,1)}, bf16[384,9,3]{0,2,1:T(4,128)(2,1)S(1)}, u32[]{:S(2)}, u32[]{:S(2)}) collective-permute-start(bf16[384,9,3]{0,2,1:T(4,128)(2,1)} %copy.74), channel_id=1, source_target_pairs={{0,1},{1,2},{2,3},{3,4},{4,5},{5,6},{6,7},{7,8},{8,9},{9,10},{10,1... | collective-permute-start | bytes 62216 | tf_op jit(solution)/shard_map/ppermute | solution.py:21
  53.2 6.1 %collective-permute-start.3 = (bf16[384,9,3]{0,2,1:T(4,128)(2,1)S(1)}, bf16[384,9,3]{0,2,1:T(4,128)(2,1)S(1)}, u32[]{:S(2)}, u32[]{:S(2)}) collective-permute-start(bf16[384,9,3]{0,2,1:T(4,128)(2,1)S(1)} %copy.75), channel_id=1, source_target_pairs={{1,0},{2,1},{3,2},{4,3},{5,4},{6,5},{7,6},{8,7},{9,8},{10,9},{11,1... | collective-permute-start | bytes 62216 | tf_op jit(solution)/shard_map/ppermute | solution.py:22
  69.4 25.0 %all-to-all-start.1 = ((bf16[32,2,2412]{2,1,0:T(2,128)(2,1)}), bf16[32,2,2412]{2,1,0:T(2,128)(2,1)}, u32[]{:S(2)}, u32[]{:S(2)}) async-start(bf16[32,2,2412]{2,1,0:T(2,128)(2,1)} %reshape.525), calls=%async_computation.1 | async-start | bytes 622592 | tf_op jit(solution)/shard_map/all_to_all | solution.py:103
  102.5 19.5 %all-to-all-start.2 = ((bf16[32,2,2412]{2,1,0:T(2,128)(2,1)}), bf16[32,2,2412]{2,1,0:T(2,128)(2,1)}, u32[]{:S(2)}, u32[]{:S(2)}) async-start(bf16[32,2,2412]{2,1,0:T(2,128)(2,1)} %reshape.527), calls=%async_computation.2 | async-start | bytes 622592 | tf_op jit(solution)/shard_map/all_to_all | solution.py:104
  113.0 27.9 %copy-start.13 = (f32[384]{0:T(512)}, f32[384]{0:T(512)S(1)}, u32[]{:S(2)}) copy-start(f32[384]{0:T(512)S(1)} %get-tuple-element.88) | copy-start | bytes 4612
  113.0 27.9 %copy-start.15 = (f32[384]{0:T(512)}, f32[384]{0:T(512)S(1)}, u32[]{:S(2)}) copy-start(f32[384]{0:T(512)S(1)} %get-tuple-element.89) | copy-start | bytes 4612
  113.0 27.9 %copy-start.17 = (f32[384]{0:T(512)}, f32[384]{0:T(512)S(1)}, u32[]{:S(2)}) copy-start(f32[384]{0:T(512)S(1)} %get-tuple-element.90) | copy-start | bytes 4612
  113.0 27.9 %copy-start.19 = (f32[384]{0:T(512)}, f32[384]{0:T(512)S(1)}, u32[]{:S(2)}) copy-start(f32[384]{0:T(512)S(1)} %get-tuple-element.91) | copy-start | bytes 4612
  140.9 11.2 %copy-start.1 = (f32[384,9,134]{2,0,1:T(8,128)}, f32[384,9,134]{2,0,1:T(8,128)S(1)}, u32[]{:S(2)}) copy-start(f32[384,9,134]{2,0,1:T(8,128)S(1)} %maximum_convert_fusion) | copy-start | bytes 5557252
  160.1 10.0 %collective-permute-start.5 = (bf16[384,3,128]{2,0,1:T(8,128)(2,1)S(1)}, bf16[384,3,128]{2,0,1:T(8,128)(2,1)S(1)}, u32[]{:S(2)}, u32[]{:S(2)}) collective-permute-start(bf16[384,3,128]{2,0,1:T(8,128)(2,1)S(1)} %copy.83), channel_id=1, source_target_pairs={{32,0},{64,32},{96,64},{128,96},{160,128},{192,160},{224,192},{256... | collective-permute-start | bytes 884744 | tf_op jit(solution)/shard_map/ppermute | solution.py:22
  162.0 12.1 %collective-permute-start.4 = (bf16[384,3,128]{2,0,1:T(8,128)(2,1)S(1)}, bf16[384,3,128]{2,0,1:T(8,128)(2,1)S(1)}, u32[]{:S(2)}, u32[]{:S(2)}) collective-permute-start(bf16[384,3,128]{2,0,1:T(8,128)(2,1)S(1)} %copy.83), channel_id=1, source_target_pairs={{0,32},{32,64},{64,96},{96,128},{128,160},{160,192},{192,224},{224... | collective-permute-start | bytes 884744 | tf_op jit(solution)/shard_map/ppermute | solution.py:21
  176.2 5.5 %collective-permute-start.6 = (bf16[384,9,3]{0,2,1:T(4,128)(2,1)}, bf16[384,9,3]{0,2,1:T(4,128)(2,1)S(1)}, u32[]{:S(2)}, u32[]{:S(2)}) collective-permute-start(bf16[384,9,3]{0,2,1:T(4,128)(2,1)} %copy.86), channel_id=1, source_target_pairs={{0,1},{1,2},{2,3},{3,4},{4,5},{5,6},{6,7},{7,8},{8,9},{9,10},{10,1... | collective-permute-start | bytes 62216 | tf_op jit(solution)/shard_map/ppermute | solution.py:21
  179.6 6.4 %collective-permute-start.7 = (bf16[384,9,3]{0,2,1:T(4,128)(2,1)S(1)}, bf16[384,9,3]{0,2,1:T(4,128)(2,1)}, u32[]{:S(2)}, u32[]{:S(2)}) collective-permute-start(bf16[384,9,3]{0,2,1:T(4,128)(2,1)S(1)} %copy.87), channel_id=1, source_target_pairs={{1,0},{2,1},{3,2},{4,3},{5,4},{6,5},{7,6},{8,7},{9,8},{10,9},{11,1... | collective-permute-start | bytes 62216 | tf_op jit(solution)/shard_map/ppermute | solution.py:22
  190.3 15.2 %copy-start.5 = (bf16[24,48,128]{2,0,1:T(8,128)(2,1)S(1)}, bf16[24,48,128]{2,0,1:T(8,128)(2,1)}, u32[]{:S(2)}) copy-start(bf16[24,48,128]{2,0,1:T(8,128)(2,1)} %copy-done.4) | copy-start | bytes 884740
  194.3 25.7 %all-to-all-start.3 = ((bf16[32,2,2412]{2,1,0:T(2,128)(2,1)}), bf16[32,2,2412]{2,1,0:T(2,128)(2,1)S(1)}, u32[]{:S(2)}, u32[]{:S(2)}) async-start(bf16[32,2,2412]{2,1,0:T(2,128)(2,1)} %reshape.529), calls=%async_computation.3 | async-start | bytes 622592 | tf_op jit(solution)/shard_map/all_to_all | solution.py:103
  225.0 40.3 %all-to-all-start.4 = ((bf16[32,2,2412]{2,1,0:T(2,128)(2,1)}), bf16[32,2,2412]{2,1,0:T(2,128)(2,1)S(1)}, u32[]{:S(2)}, u32[]{:S(2)}) async-start(bf16[32,2,2412]{2,1,0:T(2,128)(2,1)} %reshape.531), calls=%async_computation.4 | async-start | bytes 622592 | tf_op jit(solution)/shard_map/all_to_all | solution.py:104
  234.7 290.7 %all-reduce.2.cloned.1.call-start = ((), (), s32[]{:S(2)}) async-start(), calls=%async_computation.6 | async-start | bytes 172032 | tf_op jit(solution)/shard_map/psum | solution.py:150
  234.9 17.0 %copy-start.2 = (f32[384,9,134]{2,0,1:T(8,128)S(1)}, f32[384,9,134]{2,0,1:T(8,128)}, u32[]{:S(2)}) copy-start(f32[384,9,134]{2,0,1:T(8,128)} %copy-done.1) | copy-start | bytes 5557252
  252.0 11.1 %copy-start.7 = (bf16[384,3,134]{2,0,1:T(8,128)(2,1)S(1)}, bf16[384,3,134]{2,0,1:T(8,128)(2,1)}, u32[]{:S(2)}) copy-start(bf16[384,3,134]{2,0,1:T(8,128)(2,1)} %get-tuple-element.138) | copy-start | bytes 926212
  252.0 11.1 %copy-start.8 = (bf16[384,3,134]{2,0,1:T(8,128)(2,1)S(1)}, bf16[384,3,134]{2,0,1:T(8,128)(2,1)}, u32[]{:S(2)}) copy-start(bf16[384,3,134]{2,0,1:T(8,128)(2,1)} %get-tuple-element.139) | copy-start | bytes 926212
  268.2 12.6 %copy-start.14 = (f32[384]{0:T(512)S(1)}, f32[384]{0:T(512)}, u32[]{:S(2)}) copy-start(f32[384]{0:T(512)} %copy-done.13) | copy-start | bytes 4612
  268.2 12.6 %copy-start.16 = (f32[384]{0:T(512)S(1)}, f32[384]{0:T(512)}, u32[]{:S(2)}) copy-start(f32[384]{0:T(512)} %copy-done.15) | copy-start | bytes 4612
  268.2 12.6 %copy-start.18 = (f32[384]{0:T(512)S(1)}, f32[384]{0:T(512)}, u32[]{:S(2)}) copy-start(f32[384]{0:T(512)} %copy-done.17) | copy-start | bytes 4612
  268.2 12.6 %copy-start.20 = (f32[384]{0:T(512)S(1)}, f32[384]{0:T(512)}, u32[]{:S(2)}) copy-start(f32[384]{0:T(512)} %copy-done.19) | copy-start | bytes 4612
  277.1 6.9 %copy-start.22 = (f32[384]{0:T(512)S(1)}, f32[384]{0:T(512)}, u32[]{:S(2)}) copy-start(f32[384]{0:T(512)} %get-tuple-element.92) | copy-start | bytes 4612
  277.2 6.9 %copy-start.25 = (f32[384]{0:T(512)S(1)}, f32[384]{0:T(512)}, u32[]{:S(2)}) copy-start(f32[384]{0:T(512)} %get-tuple-element.93) | copy-start | bytes 4612
  277.2 6.9 %copy-start.28 = (f32[384]{0:T(512)S(1)}, f32[384]{0:T(512)}, u32[]{:S(2)}) copy-start(f32[384]{0:T(512)} %get-tuple-element.94) | copy-start | bytes 4612
  277.2 6.9 %copy-start.31 = (f32[384]{0:T(512)S(1)}, f32[384]{0:T(512)}, u32[]{:S(2)}) copy-start(f32[384]{0:T(512)} %get-tuple-element.95) | copy-start | bytes 4612
  277.2 6.9 %copy-start.34 = (f32[384]{0:T(512)S(1)}, f32[384]{0:T(512)}, u32[]{:S(2)}) copy-start(f32[384]{0:T(512)} %get-tuple-element.96) | copy-start | bytes 4612
  277.2 6.9 %copy-start.37 = (f32[384]{0:T(512)S(1)}, f32[384]{0:T(512)}, u32[]{:S(2)}) copy-start(f32[384]{0:T(512)} %get-tuple-element.97) | copy-start | bytes 4612
  277.2 6.9 %copy-start.40 = (f32[384]{0:T(512)S(1)}, f32[384]{0:T(512)}, u32[]{:S(2)}) copy-start(f32[384]{0:T(512)} %get-tuple-element.98) | copy-start | bytes 4612
  277.2 6.9 %copy-start.43 = (f32[384]{0:T(512)S(1)}, f32[384]{0:T(512)}, u32[]{:S(2)}) copy-start(f32[384]{0:T(512)} %get-tuple-element.99) | copy-start | bytes 4612
  277.2 6.9 %copy-start.46 = (f32[384]{0:T(512)S(1)}, f32[384]{0:T(512)}, u32[]{:S(2)}) copy-start(f32[384]{0:T(512)} %get-tuple-element.100) | copy-start | bytes 4612
  277.2 6.9 %copy-start.49 = (f32[384]{0:T(512)S(1)}, f32[384]{0:T(512)}, u32[]{:S(2)}) copy-start(f32[384]{0:T(512)} %get-tuple-element.101) | copy-start | bytes 4612
  277.2 6.9 %copy-start.52 = (f32[384]{0:T(512)S(1)}, f32[384]{0:T(512)}, u32[]{:S(2)}) copy-start(f32[384]{0:T(512)} %get-tuple-element.107) | copy-start | bytes 4612
  277.3 6.9 %copy-start.55 = (f32[384]{0:T(512)S(1)}, f32[384]{0:T(512)}, u32[]{:S(2)}) copy-start(f32[384]{0:T(512)} %get-tuple-element.108) | copy-start | bytes 4612
  277.3 6.9 %copy-start.58 = (f32[384]{0:T(512)S(1)}, f32[384]{0:T(512)}, u32[]{:S(2)}) copy-start(f32[384]{0:T(512)} %get-tuple-element.109) | copy-start | bytes 4612
  277.3 6.9 %copy-start.61 = (f32[384]{0:T(512)S(1)}, f32[384]{0:T(512)}, u32[]{:S(2)}) copy-start(f32[384]{0:T(512)} %get-tuple-element.102) | copy-start | bytes 4612
  277.3 6.9 %copy-start.64 = (f32[384]{0:T(512)S(1)}, f32[384]{0:T(512)}, u32[]{:S(2)}) copy-start(f32[384]{0:T(512)} %get-tuple-element.103) | copy-start | bytes 4612
  277.3 6.9 %copy-start.67 = (f32[384]{0:T(512)S(1)}, f32[384]{0:T(512)}, u32[]{:S(2)}) copy-start(f32[384]{0:T(512)} %get-tuple-element.104) | copy-start | bytes 4612
  277.3 6.9 %copy-start.70 = (f32[384]{0:T(512)S(1)}, f32[384]{0:T(512)}, u32[]{:S(2)}) copy-start(f32[384]{0:T(512)} %get-tuple-element.105) | copy-start | bytes 4612
  280.8 4.8 copy-start.3
  285.8 16.9 %copy-start.6 = (f32[1536,384]{0,1:T(8,128)S(1)}, f32[1536,384]{0,1:T(8,128)}, u32[]{:S(2)}) copy-start(f32[1536,384]{0,1:T(8,128)} %convolution_bitcast_fusion.1) | copy-start | bytes 7077892
  298.6 16.1 %all-to-all-start.5 = ((bf16[384,3,128]{2,1,0:T(4,128)(2,1)}), bf16[384,3,128]{2,1,0:T(4,128)(2,1)}, u32[]{:S(2)}, u32[]{:S(2)}) async-start(bf16[384,3,128]{2,1,0:T(4,128)(2,1)} %copy.92), calls=%async_computation.5 | async-start | bytes 786432 | tf_op jit(solution)/shard_map/all_to_all | solution.py:156
  (78 other events, 193.3 us)
Sparse Core Ops, SparseCore 0:
  263.3 262.0 all-reduce.1
where the time goes:
time: 544 us; the launch traced here: 534 us
  waiting for transfers between devices  251 us (46%)
  local copies, waits for them, and re-layouts  98.5 us (18%)
  starting transfers between devices  69.1 us (13%)
  other arithmetic  66.7 us (12%)
  blocking collectives  18.7 us (3%)
  between operations  16.7 us (3%)
  matrix products  13.5 us (2%)
    psum x1, waiting for transfers between devices, shards(): kernel_grad = lax.psum(local_terms, ('lev', 'lon'))  209 us
    unnamed x240, local copies, waits for them, and re-layouts  39.3 us
    reduce_sum x3, other arithmetic, kernel_terms(): terms.append(jnp.sum(flat * piece, axis=(1, 2)))  25.5 us
    all_to_all x2, starting transfers between devices, fold_edge(): lax.all_to_all(blocks, 'lon', split_axis=0, concat_axis=0, tiled=True)  21.6 us
    all_to_all x1, blocking collectives, shards(): lax.all_to_all(snapshot, 'lev', split_axis=1, concat_axis=0, tiled=True)  18.7 us
    ppermute x4, starting transfers between devices, padded_2(): before = lax.ppermute(last, axis, up)  17.8 us
    another operation x50, local copies, waits for them, and re-layouts, kernel_terms(): return jnp.stack(terms, axis=1)  15.1 us
    all_to_all x2, starting transfers between devices, fold_edge(): lax.all_to_all(spread[::-1], 'lon', split_axis=0, concat_axis=0, tiled=True)  14.7 us
  transfers between devices with their start and end apart: 14, of which 11 were waited for; matrix products, arithmetic and copies ran while one was open for 19% of the time, Pallas kernels for 0%

commit v1 on v0

v1 whole, which is shorter than its diff:
```python
import functools

import jax
import jax.numpy as jnp
from jax import lax
from jax.experimental import pallas as pl
from jax.experimental.pallas import tpu as pltpu
from jax.sharding import PartitionSpec as P

MESH = pl.DeviceIdType.MESH
F32 = jnp.float32
BF16 = jnp.bfloat16
TAPS = 7
REACH = 3
W = 128
SUB = 8

epsilon = 1e-06
root_half = 0.7071067811865476
inv_root_tau = 0.3989422804014327


class Dims:
    def __init__(self, levs, lons, channels, rows, hidden):
        self.levs, self.lons, self.channels, self.rows, self.hidden = levs, lons, channels, rows, hidden
        self.cl = channels // levs
        self.tile = rows // levs
        self.used = self.tile * self.cl
        self.block = -(-(self.used + 2 * self.tile) // 16) * 16
        self.groups = self.cl // SUB
        self.step = max(r for r in (8, 6, 4, 3) if rows % r == 0)
        self.packs = -(-rows // 32)
        self.core = 2
        self.zhi = 4 if lons == 32 else 2
        self.x = lons // (self.core * self.zhi)
        self.first = self.x * self.core


def lane_iota(shape=(SUB, W)):
    return lax.broadcasted_iota(jnp.int32, shape, 1)


def lev_peer(d, me, offset):
    return lax.rem(me + offset, d.levs)


def lon_targets(d):
    me = lax.axis_index("lon")
    n = d.lons
    mirror = n - 1 - me
    right, left = lax.rem(me + 1, n), lax.rem(me + n - 1, n)
    return me, (right, left), (mirror, lax.rem(mirror + 1, n), lax.rem(mirror + n - 1, n))


def signal(sem, where):
    pl.semaphore_signal(sem, inc=1, device_id=where, device_id_type=MESH)


def greet(d, sem):
    lev = lax.axis_index("lev")
    me, sides, mirrors = lon_targets(d)

    @pl.loop(1, d.levs)
    def _(s):
        signal(sem, {"lev": lev_peer(d, lev, s)})

    for side in sides:
        signal(sem, {"lon": side})
    for mirror in mirrors:

        @pl.when(mirror != me)
        def _(mirror=mirror):
            signal(sem, {"lon": mirror})


def met(d, sem, more=0):
    me, _, mirrors = lon_targets(d)
    own = sum(jnp.where(mirror == me, 1, 0) for mirror in mirrors)
    pl.semaphore_wait(sem, d.levs - 1 + 2 + len(mirrors) + more - own)


def edge_copies(d, hs, hr, fs, fr, sems):
    me, sides, mirrors = lon_targets(d)
    send, recv = sems
    for j, side in enumerate(sides):
        yield None, pltpu.make_async_remote_copy(
            src_ref=hs.at[j], dst_ref=hr.at[j], send_sem=send.at[j], recv_sem=recv.at[j],
            device_id={"lon": side}, device_id_type=MESH,
        ), None
    for j, mirror in enumerate(mirrors):
        yield mirror != me, pltpu.make_async_remote_copy(
            src_ref=fs, dst_ref=fr.at[j], send_sem=send.at[2 + j], recv_sem=recv.at[2 + j],
            device_id={"lon": mirror}, device_id_type=MESH,
        ), pltpu.make_async_copy(fs, fr.at[j], recv.at[2 + j])


def edge_start(d, *refs):
    for away, remote, own in edge_copies(d, *refs):
        if away is None:
            remote.start()
        else:
            pl.when(away)(remote.start)
            pl.when(jnp.logical_not(away))(own.start)


def edge_wait(d, *refs):
    for away, remote, own in edge_copies(d, *refs):
        if away is None:
            remote.wait()
        else:
            pl.when(away)(remote.wait)
            pl.when(jnp.logical_not(away))(own.wait)


def block_copy(d, me, offset, src, dst, send, recv, arriving=False):
    peer = lev_peer(d, me, offset)
    return pltpu.make_async_remote_copy(
        src_ref=src.at[peer],
        dst_ref=dst.at[peer if arriving else me],
        send_sem=send.at[peer],
        recv_sem=recv.at[peer if arriving else me],
        device_id={"lev": peer},
        device_id_type=MESH,
    )


def blocks_start(d, src, dst, send, recv):
    me = lax.axis_index("lev")

    @pl.loop(1, d.levs)
    def _(s):
        block_copy(d, me, s, src, dst, send, recv).start()

    dst[me] = src[me]


def blocks_arrive(d, src, dst, send, recv):
    me = lax.axis_index("lev")

    @pl.loop(1, d.levs)
    def _(s):
        block_copy(d, me, s, src, dst, send, recv, True).wait_recv()


def blocks_sent(d, src, dst, send, recv):
    me = lax.axis_index("lev")

    @pl.loop(1, d.levs)
    def _(s):
        block_copy(d, me, s, src, dst, send, recv).wait_send()


def pack_edges(d, rows, hs, fs, tail):
    slot = lane_iota() >> 2

    @pl.loop(0, d.groups)
    def _(g):
        for q in range(d.packs):
            last = jnp.zeros((SUB, W), F32)
            lead = jnp.zeros((SUB, W), F32)
            for r in range(32 * q, min(32 * q + 32, d.rows)):
                s = r - 32 * q
                v = rows[pl.ds(pl.multiple_of(r * d.cl + g * SUB, SUB), SUB), :]
                here = slot == s
                last = jnp.where(here, pltpu.roll(v, (4 * s - (W - REACH)) % W, 1), last)
                lead = jnp.where(here, pltpu.roll(v, 4 * s, 1) if s else v, lead)
            at = pl.ds(pl.multiple_of(q * d.cl + g * SUB, SUB), SUB)
            tail[0, at, :] = last
            tail[1, at, :] = lead

    hs[...] = tail[:, : hs.shape[1], :].astype(BF16)
    north = (d.rows - REACH) * d.cl
    fs[: REACH * d.cl, :] = rows[north : north + REACH * d.cl, :].astype(BF16)


def store_shifts(x, left, right, lane, put):
    put(REACH, x)
    for k in range(1, REACH + 1):
        put(REACH - k, pltpu.roll(jnp.where(lane >= W - k, left, x), k, 1))
        put(REACH + k, pltpu.roll(jnp.where(lane < k, right, x), W - k, 1))


def build_shifts(d, rows, hr, halo, out):
    halo[:, : hr.shape[1], :] = hr[...].astype(F32)
    lane = lane_iota()

    @pl.loop(0, d.groups)
    def _(g):
        for r in range(d.rows):
            q, s = divmod(r, 32)
            at = pl.ds(pl.multiple_of(q * d.cl + g * SUB, SUB), SUB)
            left = pltpu.roll(halo[0, at, :], (W - REACH - 4 * s) % W, 1)
            right = pltpu.roll(halo[1, at, :], (W - 4 * s) % W, 1) if s else halo[1, at, :]
            x = rows[pl.ds(pl.multiple_of(r * d.cl + g * SUB, SUB), SUB), :]
            to = pl.ds(pl.multiple_of((r + REACH) * d.cl + g * SUB, SUB), SUB)

            def put(b, value, to=to):
                out[b, to, :] = value

            store_shifts(x, left, right, lane, put)


def fold_shifts(d, fr, out, base):
    count = REACH * d.cl
    flip = lax.broadcasted_iota(jnp.int32, (W, W), 0) + lax.broadcasted_iota(jnp.int32, (W, W), 1) == W - 1
    flip = flip.astype(F32).astype(BF16)
    centre, left, right = (jnp.dot(fr[j], flip, preferred_element_type=F32) for j in range(3))
    lane = lane_iota()
    for m in range(REACH):
        for g in range(d.groups):
            src = (REACH - 1 - m) * d.cl + g * SUB
            to = base + m * d.cl + g * SUB

            def put(b, value, to=to):
                out[b, to : to + SUB, :] = value

            store_shifts(centre[src : src + SUB], left[src : src + SUB], right[src : src + SUB], lane, put)


def correlate(d, image, weights, out, flipped):
    blocks = d.rows // d.step

    @pl.loop(0, blocks * d.groups)
    def _(n):
        g = lax.rem(n, d.groups)
        top = n // d.groups * d.step
        acc = [jnp.zeros((SUB, W), F32) for _ in range(d.step)]
        for b in range(TAPS):
            near = TAPS - 1 - b if flipped else b
            lines = [
                image[near, pl.ds(pl.multiple_of((top + t) * d.cl + g * SUB, SUB), SUB), :]
                for t in range(d.step + TAPS - 1)
            ]
            for a in range(TAPS):
                w = weights[a * TAPS + b, pl.ds(pl.multiple_of(g * SUB, SUB), SUB), :]
                down = TAPS - 1 - a if flipped else a
                acc = [acc[i] + w * lines[i + down] for i in range(d.step)]
        for i in range(d.step):
            out[pl.ds(pl.multiple_of((top + i) * d.cl + g * SUB, SUB), SUB), :] = acc[i]


def tap_products(d, image, flat, grad):
    lane = lane_iota()
    grad[...] = jnp.zeros_like(grad)

    @pl.loop(0, TAPS * d.groups)
    def _(n):
        b = lax.rem(n, TAPS)
        g = n // TAPS
        acc = [jnp.zeros((SUB, W), F32) for _ in range(TAPS)]
        for block in range(d.rows // d.step):
            top = block * d.step
            lines = [
                image[b, pl.ds(pl.multiple_of((top + t) * d.cl + g * SUB, SUB), SUB), :]
                for t in range(d.step + TAPS - 1)
            ]
            for i in range(d.step):
                v = flat[pl.ds(pl.multiple_of((top + i) * d.cl + g * SUB, SUB), SUB), :]
                acc = [acc[a] + v * lines[i + a] for a in range(TAPS)]
        at = pl.ds(pl.multiple_of(g * SUB, SUB), SUB)
        total = grad[at, :]
        for a in range(TAPS):
            total = jnp.where(lane == a * TAPS + b, jnp.sum(acc[a], axis=1, keepdims=True), total)
        grad[at, :] = total


def forward_kernel(d, snap, kern, cbuf, rbuf, shifted, weights,
                   rows, conv, pad32, wide, tail, hs, hr, fs, fr, rs, cs,
                   edge_send, edge_recv, r_send, r_recv, c_send, c_recv):
    barrier = pltpu.get_barrier_semaphore()
    greet(d, barrier)
    lev = lax.axis_index("lev")
    for c in range(d.cl):
        rows[pl.ds(c, d.rows, stride=d.cl), :] = snap[c].astype(F32)
    fs[...] = jnp.zeros_like(fs)
    pack_edges(d, rows, hs, fs, tail)
    for k in range(d.levs):
        rs[k, : d.used, :] = rows[k * d.used : (k + 1) * d.used, :].astype(BF16)
        rs[k, d.used :, :] = jnp.zeros((d.block - d.used, W), BF16)
    met(d, barrier)
    edge = (hs, hr, fs, fr, (edge_send, edge_recv))
    edge_start(d, *edge)
    blocks_start(d, rs, rbuf, r_send, r_recv)

    wide[...] = kern[...].astype(F32)
    mine = wide[pl.ds(pl.multiple_of(lev * d.cl, SUB), d.cl), :]
    for t in range(TAPS * TAPS):
        weights[t] = jnp.broadcast_to(mine[:, t : t + 1], (d.cl, W))
    for b in range(TAPS):
        shifted[b, : REACH * d.cl, :] = jnp.zeros((REACH * d.cl, W), F32)

    edge_wait(d, *edge)
    build_shifts(d, rows, hr, tail, shifted)
    fold_shifts(d, fr, shifted, (REACH + d.rows) * d.cl)
    correlate(d, shifted, weights, conv, False)

    sub = lax.broadcasted_iota(jnp.int32, (d.block - d.used, W), 0)

    @pl.loop(0, d.levs)
    def _(k):
        offsets = jnp.zeros((d.block - d.used, W), F32)
        for r in range(d.tile):
            v = conv[pl.ds(pl.multiple_of(k * d.used + r * d.cl, SUB), d.cl), :]
            mean = jnp.sum(v, axis=0, keepdims=True) * (1.0 / d.cl)
            high = mean.astype(BF16).astype(F32)
            low = (mean - high).astype(BF16).astype(F32)
            pad32[r * d.cl : (r + 1) * d.cl, :] = v - (high + low)
            offsets = jnp.where(sub == 2 * r, high, jnp.where(sub == 2 * r + 1, low, offsets))
        pad32[d.used :, :] = offsets
        cs[k] = pad32[...].astype(BF16)

    blocks_start(d, cs, cbuf, c_send, c_recv)
    blocks_arrive(d, rs, rbuf, r_send, r_recv)
    blocks_arrive(d, cs, cbuf, c_send, c_recv)
    blocks_sent(d, rs, rbuf, r_send, r_recv)
    blocks_sent(d, cs, cbuf, c_send, c_recv)


def column_of(vector, out):
    for j in range(vector.shape[0]):
        n = vector.shape[1]
        line = jnp.broadcast_to(vector[j : j + 1, :], (W, n))
        out[j * n : (j + 1) * n, :] = jnp.transpose(line)


def cell_kernel(d, cbuf, rbuf, cot, mask, gain, shift, w_in, w_out, result, dsend, usend,
                gains, shifts, normed, rstds, lifted, upstream, projected, d_lifted, blocks):
    column_of(gain[...], gains)
    column_of(shift[...], shifts)
    for k in range(d.levs):
        v = cbuf[k].astype(F32)
        for r in range(d.tile):
            at = d.used + 2 * r
            normed[r, k * d.cl : (k + 1) * d.cl, :] = v[r * d.cl : (r + 1) * d.cl] + (v[at : at + 1] + v[at + 1 : at + 2])
    wet = mask[...].astype(F32)
    inv = 1.0 / d.channels
    for r in range(d.tile):
        v = normed[r]
        v = v - jnp.sum(v, axis=0, keepdims=True) * inv
        spread = jnp.sum(v * v, axis=0, keepdims=True) * inv
        rstd = lax.rsqrt(spread + epsilon)
        v = v * rstd
        normed[r] = v
        rstds[r : r + 1, :] = rstd
        cells = pl.ds(r * W, W)
        lifted[cells, :] = jnp.transpose(v * gains[...] + shifts[...]).astype(BF16)
        up = cot[r].astype(F32) * wet[r : r + 1, :]
        upstream[cells, :] = jnp.transpose(up).astype(BF16)
        for k in range(d.levs):
            blocks[k, r * d.cl : (r + 1) * d.cl, :] = up[k * d.cl : (k + 1) * d.cl]
    for k in range(d.levs):
        blocks[k, d.used :, :] = jnp.zeros((d.block - d.used, W), F32)
    usend[...] = blocks[...].astype(BF16)

    chunk = 256
    for n in range(d.hidden // chunk):
        f = slice(n * chunk, (n + 1) * chunk)
        hidden = jnp.dot(lifted[...], w_in[:, f], preferred_element_type=F32)
        d_active = lax.dot_general(upstream[...], w_out[f, :], (((1,), (1,)), ((), ())), preferred_element_type=F32)
        share = 0.5 * (1.0 + lax.erf(hidden * root_half))
        active = (hidden * share).astype(BF16)
        slope = share + hidden * jnp.exp(-0.5 * hidden * hidden) * inv_root_tau
        d_hidden = (d_active * slope).astype(BF16)
        p = jnp.dot(active, w_out[f, :], preferred_element_type=F32)
        q = lax.dot_general(w_in[:, f], d_hidden, (((1,), (1,)), ((), ())), preferred_element_type=F32)
        if n == 0:
            projected[...] = p
            d_lifted[...] = q
        else:
            projected[...] += p
            d_lifted[...] += q

    for k in range(d.levs):
        blocks[k] = rbuf[k].astype(F32)
    for r in range(d.tile):
        cells = slice(r * W, (r + 1) * W)
        out = jnp.transpose(projected[cells, :])
        for k in range(d.levs):
            part = slice(k * d.cl, (k + 1) * d.cl)
            d_lifted_part = blocks[k, r * d.cl : (r + 1) * d.cl, :] + out[part]
            shifts[part, :] = wet[r : r + 1, :] * d_lifted_part
        result[r] = shifts[...].astype(BF16)
        dn = d_lifted[:, cells] * gains[...]
        v = normed[r]
        mean = jnp.sum(dn, axis=0, keepdims=True) * inv
        along = jnp.sum(dn * v, axis=0, keepdims=True) * inv
        dc = rstds[r : r + 1, :] * (dn - mean - v * along)
        normed[r] = dc
    for r in range(d.tile):
        for k in range(d.levs):
            blocks[k, r * d.cl : (r + 1) * d.cl, :] = normed[r, k * d.cl : (k + 1) * d.cl, :]
    dsend[...] = blocks[...].astype(BF16)


def first_peer(d, lon, offset):
    z = lax.rem(lon // d.core, d.zhi)
    mine = lon // (d.core * d.zhi) * d.core + lax.rem(lon, d.core)
    theirs = lax.rem(mine + offset, d.first)
    peer = (theirs // d.core * d.zhi + z) * d.core + lax.rem(theirs, d.core)
    return mine, theirs, peer


def second_peer(d, lon, offset):
    mine = lax.rem(lon // d.core, d.zhi)
    theirs = lax.rem(mine + offset, d.zhi)
    return mine, theirs, lon + (theirs - mine) * d.core


def share_copy(d, peers, count, offset, src, dst, send, recv, arriving=False):
    mine, theirs, peer = peers(d, lax.axis_index("lon"), offset)
    return pltpu.make_async_remote_copy(
        src_ref=src, dst_ref=dst.at[theirs if arriving else mine], send_sem=send.at[theirs],
        recv_sem=recv.at[theirs if arriving else mine], device_id={"lon": peer}, device_id_type=MESH,
    )


def share_start(d, peers, count, src, dst, send, recv):
    mine, _, _ = peers(d, lax.axis_index("lon"), 1)
    for s in range(1, count):
        share_copy(d, peers, count, s, src, dst, send, recv).start()
    dst[mine] = src[...]


def share_wait(d, peers, count, src, dst, send, recv):
    for s in range(1, count):
        share_copy(d, peers, count, s, src, dst, send, recv, True).wait_recv()
    for s in range(1, count):
        share_copy(d, peers, count, s, src, dst, send, recv).wait_send()


def gather_copy(d, offset, src, dst, send, recv, arriving=False):
    me = lax.axis_index("lev")
    peer = lev_peer(d, me, offset)
    return pltpu.make_async_remote_copy(
        src_ref=src, dst_ref=dst.at[peer if arriving else me], send_sem=send.at[peer],
        recv_sem=recv.at[peer if arriving else me], device_id={"lev": peer}, device_id_type=MESH,
    )


def backward_kernel(d, dsend, usend, shifted, weights, out, grads,
                    rows, image, fold, tail, sums, hs, hr, fs, fr, dbuf, ubuf, grad, part1, total1, part2, total2,
                    edge_send, edge_recv, d_send, d_recv, u_send, u_recv, p1s, p1r, p2s, p2r, gs, gr):
    barrier = pltpu.get_barrier_semaphore()
    greet(d, barrier)
    lon = lax.axis_index("lon")
    lev = lax.axis_index("lev")
    for s in range(1, d.first):
        signal(barrier, {"lon": first_peer(d, lon, s)[2]})
    for s in range(1, d.zhi):
        signal(barrier, {"lon": second_peer(d, lon, s)[2]})
    fs[...] = jnp.zeros_like(fs)
    for b in range(TAPS):
        image[b, : REACH * d.cl, :] = jnp.zeros((REACH * d.cl, W), F32)
        image[b, (REACH + d.rows) * d.cl :, :] = jnp.zeros((REACH * d.cl, W), F32)
    met(d, barrier, d.first - 1 + d.zhi - 1)
    blocks_start(d, dsend, dbuf, d_send, d_recv)
    blocks_start(d, usend, ubuf, u_send, u_recv)

    blocks_arrive(d, dsend, dbuf, d_send, d_recv)
    for k in range(d.levs):
        rows[k * d.used : (k + 1) * d.used, :] = dbuf[k, : d.used, :].astype(F32)
    pack_edges(d, rows, hs, fs, tail)
    edge = (hs, hr, fs, fr, (edge_send, edge_recv))
    edge_start(d, *edge)
    tap_products(d, shifted, rows, grad)
    first = (d, first_peer, d.first, grad, part1, p1s, p1r)
    share_start(*first)

    edge_wait(d, *edge)
    build_shifts(d, rows, hr, tail, image)
    fold_shifts(d, fr, fold, 0)

    share_wait(*first)
    total1[...] = sum(part1[i] for i in range(d.first))
    second = (d, second_peer, d.zhi, total1, part2, p2s, p2r)
    share_start(*second)

    correlate(d, image, weights, sums, True)

    share_wait(*second)
    total2[...] = sum(part2[i] for i in range(d.zhi))
    for s in range(1, d.levs):
        gather_copy(d, s, total2, grads, gs, gr).start()
    grads[lev] = total2[...]

    for m in range(REACH):
        for g in range(d.groups):
            at = (d.rows - 1 - m) * d.cl + g * SUB
            acc = sums[at : at + SUB, :]
            for k in range(REACH - m):
                for b in range(TAPS):
                    w = weights[(REACH + 1 + m + k) * TAPS + b, g * SUB : (g + 1) * SUB, :]
                    acc = acc + w * fold[b, k * d.cl + g * SUB : k * d.cl + (g + 1) * SUB, :]
            sums[at : at + SUB, :] = acc
    blocks_arrive(d, usend, ubuf, u_send, u_recv)
    for k in range(d.levs):
        part = slice(k * d.used, (k + 1) * d.used)
        sums[part, :] = sums[part, :] + ubuf[k, : d.used, :].astype(F32)
    for c in range(d.cl):
        out[c] = sums[pl.ds(c, d.rows, stride=d.cl), :].astype(BF16)

    for s in range(1, d.levs):
        gather_copy(d, s, total2, grads, gs, gr, True).wait_recv()
    for s in range(1, d.levs):
        gather_copy(d, s, total2, grads, gs, gr).wait_send()
    blocks_sent(d, dsend, dbuf, d_send, d_recv)
    blocks_sent(d, usend, ubuf, u_send, u_recv)


VMEM = pl.BlockSpec(memory_space=pltpu.VMEM)
DMA = pltpu.SemaphoreType.DMA
LIMIT = 60 * 1024 * 1024


def params(number):
    return pltpu.CompilerParams(collective_id=number, has_side_effects=True, vmem_limit_bytes=LIMIT)


def shards(snapshot, cotangent, ocean_mask, kernel, norm_gain, norm_shift, weight_in, weight_out):
    levs, lons = lax.axis_size("lev"), lax.axis_size("lon")
    cl, rows, _ = snapshot.shape
    d = Dims(levs, lons, cl * levs, rows, weight_in.shape[1])
    sds = jax.ShapeDtypeStruct
    blocks = (d.levs, d.block, W)
    flat = (d.rows * d.cl, W)
    image = (TAPS, (d.rows + 2 * REACH) * d.cl, W)
    halo = (2, -(-d.packs * d.cl // 16) * 16, W)
    north = (-(-REACH * d.cl // 16) * 16, W)
    edge_scratch = [
        pltpu.VMEM(halo, BF16), pltpu.VMEM(halo, BF16), pltpu.VMEM(north, BF16), pltpu.VMEM((3, *north), BF16),
    ]
    cbuf, rbuf, shifted, weights = pl.pallas_call(
        functools.partial(forward_kernel, d),
        name="forward",
        out_shape=(sds(blocks, BF16), sds(blocks, BF16), sds(image, F32), sds((TAPS * TAPS, d.cl, W), F32)),
        in_specs=[VMEM] * 2,
        out_specs=(VMEM,) * 4,
        scratch_shapes=[
            pltpu.VMEM(flat, F32), pltpu.VMEM(flat, F32), pltpu.VMEM((d.block, W), F32),
            pltpu.VMEM((d.channels, TAPS * TAPS), F32), pltpu.VMEM(halo, F32), *edge_scratch,
            pltpu.VMEM(blocks, BF16), pltpu.VMEM(blocks, BF16),
            DMA((5,)), DMA((5,)), *[DMA((d.levs,))] * 4,
        ],
        compiler_params=params(0),
    )(snapshot, kernel)

    cells = d.tile * W
    result, dsend, usend = pl.pallas_call(
        functools.partial(cell_kernel, d),
        name="cells",
        out_shape=(sds((d.tile, d.channels, W), BF16), sds(blocks, BF16), sds(blocks, BF16)),
        in_specs=[VMEM] * 8,
        out_specs=(VMEM,) * 3,
        scratch_shapes=[
            pltpu.VMEM((d.channels, W), F32), pltpu.VMEM((d.channels, W), F32),
            pltpu.VMEM((d.tile, d.channels, W), F32), pltpu.VMEM((d.tile, W), F32),
            pltpu.VMEM((cells, d.channels), BF16), pltpu.VMEM((cells, d.channels), BF16),
            pltpu.VMEM((cells, d.channels), F32), pltpu.VMEM((d.channels, cells), F32),
            pltpu.VMEM(blocks, F32),
        ],
        compiler_params=pltpu.CompilerParams(vmem_limit_bytes=LIMIT),
    )(
        cbuf, rbuf, jnp.swapaxes(cotangent, 0, 1), ocean_mask,
        norm_gain.reshape(-1, min(W, d.channels)), norm_shift.reshape(-1, min(W, d.channels)), weight_in, weight_out,
    )

    share = (d.cl, W)
    d_snapshot, grads = pl.pallas_call(
        functools.partial(backward_kernel, d),
        name="backward",
        out_shape=(sds((d.cl, d.rows, W), BF16), sds((d.levs, *share), F32)),
        in_specs=[VMEM] * 4,
        out_specs=(VMEM,) * 2,
        scratch_shapes=[
            pltpu.VMEM(flat, F32), pltpu.VMEM(image, F32), pltpu.VMEM((TAPS, REACH * d.cl, W), F32),
            pltpu.VMEM(halo, F32), pltpu.VMEM(flat, F32), *edge_scratch,
            pltpu.VMEM(blocks, BF16), pltpu.VMEM(blocks, BF16),
            pltpu.VMEM(share, F32), pltpu.VMEM((d.first, *share), F32), pltpu.VMEM(share, F32),
            pltpu.VMEM((d.zhi, *share), F32), pltpu.VMEM(share, F32),
            DMA((5,)), DMA((5,)), *[DMA((d.levs,))] * 4,
            DMA((d.first,)), DMA((d.first,)), DMA((d.zhi,)), DMA((d.zhi,)), DMA((d.levs,)), DMA((d.levs,)),
        ],
        compiler_params=params(1),
    )(dsend, usend, shifted, weights)
    kernel_grad = grads.reshape(d.channels, W)[:, : TAPS * TAPS]
    return jnp.swapaxes(result, 0, 1), d_snapshot, kernel_grad


def solution(mesh):
    placed = (
        P("lev", None, "lon"),
        P(None, "lev", "lon"),
        P("lev", "lon"),
        P(),
        P(),
        P(),
        P(),
        P(),
    )
    return jax.shard_map(
        shards,
        mesh=mesh,
        in_specs=placed,
        out_specs=(P(None, "lev", "lon"), P("lev", None, "lon"), P()),
        check_vma=False,
    )
```

time: 544 us -> 106 us (0.19); the launches traced: 534 us -> 106 us
  waiting for transfers between devices: 251 us -> 0 us
  Pallas kernels: 0 us -> 101 us
  local copies, waits for them, and re-layouts: 98.5 us -> 4.91 us
  starting transfers between devices: 69.1 us -> 0 us
  other arithmetic: 66.7 us -> 0 us
  blocking collectives: 18.7 us -> 0 us
  between operations: 16.7 us -> 0.65 us
  matrix products: 13.5 us -> 0 us
    psum x1 -> x0, waiting for transfers between devices: 209 us -> none  [shards(): kernel_grad = lax.psum(local_terms, ('lev', 'lon'))]
    pallas_call x0 -> x3, Pallas kernels: none -> 101 us  [the longest x1 49.8 us: shards(): pl.pallas_call(functools.partial(backward_kernel, d), name='backward', ou...]
    all_to_all x5 -> x0, starting transfers between devices: 40.5 us -> none  [the longest x2 21.6 us: fold_edge(): lax.all_to_all(blocks, 'lon', split_axis=0, concat_axis=0, tiled=True)]
    reduce_sum x6 -> x0, other arithmetic: 36.5 us -> none  [the longest x3 25.5 us: kernel_terms(): terms.append(jnp.sum(flat * piece, axis=(1, 2)))]
    unnamed x240 -> x3, local copies, waits for them, and re-layouts: 39.3 us -> 4.91 us
    ppermute x8 -> x0, starting transfers between devices: 28.4 us -> none  [the longest x4 17.8 us: padded_2(): before = lax.ppermute(last, axis, up)]
    ppermute x8 -> x0, waiting for transfers between devices: 22.8 us -> none  [the longest x4 14.2 us: padded_2(): after = lax.ppermute(leading, axis, down)]
    slice x33 -> x0, local copies, waits for them, and re-layouts: 22.4 us -> none  [the longest x23 13.6 us: fold_term(): piece = fold_rows[:, source, col_off:col_off + width].astype(jnp.float32)]
  transfers between devices with their start and end apart: 14 -> 0, of which waited for: 11 -> 0; matrix products, arithmetic and copies ran while one was open for 19% -> 0% of each run, Pallas kernels for 0% -> 0%
where the time goes in v1:
time: 106 us
  Pallas kernels  101 us (95%)
  local copies, waits for them, and re-layouts  4.91 us (5%)
    pallas_call x1, Pallas kernels, shards(): pl.pallas_call(functools.partial(backward_kernel, d), name='backward', ou...  49.8 us
    pallas_call x1, Pallas kernels, shards(): pl.pallas_call(functools.partial(forward_kernel, d), name='forward', out_...  44.1 us
    pallas_call x1, Pallas kernels, shards(): pl.pallas_call(functools.partial(cell_kernel, d), name='cells', out_shape...  6.7 us
    unnamed x3, local copies, waits for them, and re-layouts  4.91 us

profile of v1, /device:TPU:1, one launch (start us, length us, event | category | flops | bytes accessed | tf_op | source)
XLA Modules:
  0.0 106.2 jit_solution(5868795312557474770)
XLA Ops:
  0.6 1.5 %copy.11.kern = bf16[384,49]{1,0:T(8,128)(2,1)} copy(bf16[384,49]{0,1:T(8,128)(2,1)} %param.11) | data formatting | bytes 75264 | tf_op args[3]
  2.2 44.1 %forward.1 = (bf16[16,80,128]{2,1,0:T(8,128)(2,1)}, bf16[16,80,128]{2,1,0:T(8,128)(2,1)}, f32[7,1296,128]{2,1,0:T(8,128)}, f32[49,24,128]{2,1,0:T(8,128)}) custom-call(bf16[24,48,128]{2,1,0:T(8,128)(2,1)} %snap.1, bf16[384,49]{1,0:T(8,128)(2,1)} %copy.11.kern), custom_call_target="tpu_custom_call" | custom-call | tf_op jit(solution)/shard_map/forward/pallas_call | solution.py:532
  46.3 6.7 %cells.1 = (bf16[3,384,128]{2,1,0:T(8,128)(2,1)}, bf16[16,80,128]{2,1,0:T(8,128)(2,1)}, bf16[16,80,128]{2,1,0:T(8,128)(2,1)}) custom-call(bf16[16,80,128]{2,1,0:T(8,128)(2,1)} %get-tuple-element.12.cbuf, bf16[16,80,128]{2,1,0:T(8,128)(2,1)} %get-tuple-element.13.rbuf, bf16[3,384,128]{2,1,0:T(8,128)(2,1)} %bitcast.6, s32[3,128]{1,0:T(4,128)} %mask.1, ...), custom_call_target="tpu_custom_call" | custom-call | tf_op jit(solution)/shard_map/cells/pallas_call | solution.py:548
  53.0 49.8 %backward.1 = (bf16[24,48,128]{2,1,0:T(8,128)(2,1)}, f32[16,24,128]{2,1,0:T(8,128)}) custom-call(bf16[16,80,128]{2,1,0:T(8,128)(2,1)} %get-tuple-element.15.dsend, bf16[16,80,128]{2,1,0:T(8,128)(2,1)} %get-tuple-element.16.usend, f32[7,1296,128]{2,1,0:T(8,128)} %get-tuple-element.17.shifted, f32[49,24,128]{2,1,0:T(8,128)} %get-tuple-element.18.weights), custom_call_target="tpu_custom_call" | custom-call | tf_op jit(solution)/shard_map/backward/pallas_call | solution.py:568
  102.8 1.7 %copy.13 = f32[384,49]{0,1:T(8,128)} copy(f32[384,49]{1,0:T(8,128)} %bitcast.7) | data formatting | bytes 150528
  104.5 1.7 %copy.15 = bf16[24,48,128]{2,1,0:T(8,128)(2,1)} copy(bf16[24,48,128]{2,1,0:T(8,128)(2,1)} %get-tuple-element.25) | data formatting | bytes 589824

commit v2 on v1

v2 whole, which is shorter than its diff:
```python
import contextlib
import functools

import jax
import jax.numpy as jnp
from jax import lax
from jax.experimental import pallas as pl
from jax.experimental.pallas import tpu as pltpu
from jax.sharding import PartitionSpec as P

MESH = pl.DeviceIdType.MESH
F32 = jnp.float32
BF16 = jnp.bfloat16
TAPS = 7
REACH = 3
W = 128
SUB = 8

epsilon = 1e-06
root_half = 0.7071067811865476
inv_root_tau = 0.3989422804014327


TRACE = False


def phase(name):
    return jax.named_scope(name) if TRACE else contextlib.nullcontext()


class Dims:
    def __init__(self, levs, lons, channels, rows, hidden):
        self.levs, self.lons, self.channels, self.rows, self.hidden = levs, lons, channels, rows, hidden
        self.cl = channels // levs
        self.tile = rows // levs
        self.used = self.tile * self.cl
        self.block = -(-(self.used + 2 * self.tile) // 16) * 16
        self.groups = self.cl // SUB
        self.step = max(r for r in (8, 6, 4, 3) if rows % r == 0)
        self.packs = -(-rows // 32)
        self.core = 2
        self.zhi = 4 if lons == 32 else 2
        self.x = lons // (self.core * self.zhi)
        self.first = self.x * self.core


def lane_iota(shape=(SUB, W)):
    return lax.broadcasted_iota(jnp.int32, shape, 1)


def lev_peer(d, me, offset):
    return lax.rem(me + offset, d.levs)


def lon_targets(d):
    me = lax.axis_index("lon")
    n = d.lons
    mirror = n - 1 - me
    right, left = lax.rem(me + 1, n), lax.rem(me + n - 1, n)
    return me, (right, left), (mirror, lax.rem(mirror + 1, n), lax.rem(mirror + n - 1, n))


def signal(sem, where):
    pl.semaphore_signal(sem, inc=1, device_id=where, device_id_type=MESH)


def greet(d, sem):
    lev = lax.axis_index("lev")
    me, sides, mirrors = lon_targets(d)

    @pl.loop(1, d.levs)
    def _(s):
        signal(sem, {"lev": lev_peer(d, lev, s)})

    for side in sides:
        signal(sem, {"lon": side})
    for mirror in mirrors:

        @pl.when(mirror != me)
        def _(mirror=mirror):
            signal(sem, {"lon": mirror})


def met(d, sem, more=0):
    me, _, mirrors = lon_targets(d)
    own = sum(jnp.where(mirror == me, 1, 0) for mirror in mirrors)
    pl.semaphore_wait(sem, d.levs - 1 + 2 + len(mirrors) + more - own)


def edge_copies(d, hs, hr, fs, fr, sems):
    me, sides, mirrors = lon_targets(d)
    send, recv = sems
    for j, side in enumerate(sides):
        yield None, pltpu.make_async_remote_copy(
            src_ref=hs.at[j], dst_ref=hr.at[j], send_sem=send.at[j], recv_sem=recv.at[j],
            device_id={"lon": side}, device_id_type=MESH,
        ), None
    for j, mirror in enumerate(mirrors):
        yield mirror != me, pltpu.make_async_remote_copy(
            src_ref=fs, dst_ref=fr.at[j], send_sem=send.at[2 + j], recv_sem=recv.at[2 + j],
            device_id={"lon": mirror}, device_id_type=MESH,
        ), pltpu.make_async_copy(fs, fr.at[j], recv.at[2 + j])


def edge_start(d, *refs):
    for away, remote, own in edge_copies(d, *refs):
        if away is None:
            remote.start()
        else:
            pl.when(away)(remote.start)
            pl.when(jnp.logical_not(away))(own.start)


def edge_wait(d, *refs):
    for away, remote, own in edge_copies(d, *refs):
        if away is None:
            remote.wait()
        else:
            pl.when(away)(remote.wait)
            pl.when(jnp.logical_not(away))(own.wait)


def block_copy(d, me, offset, src, dst, send, recv, arriving=False):
    peer = lev_peer(d, me, offset)
    return pltpu.make_async_remote_copy(
        src_ref=src.at[peer],
        dst_ref=dst.at[peer if arriving else me],
        send_sem=send.at[peer],
        recv_sem=recv.at[peer if arriving else me],
        device_id={"lev": peer},
        device_id_type=MESH,
    )


def blocks_start(d, src, dst, send, recv):
    me = lax.axis_index("lev")

    @pl.loop(1, d.levs)
    def _(s):
        block_copy(d, me, s, src, dst, send, recv).start()

    dst[me] = src[me]


def blocks_arrive(d, src, dst, send, recv):
    me = lax.axis_index("lev")

    @pl.loop(1, d.levs)
    def _(s):
        block_copy(d, me, s, src, dst, send, recv, True).wait_recv()


def blocks_sent(d, src, dst, send, recv):
    me = lax.axis_index("lev")

    @pl.loop(1, d.levs)
    def _(s):
        block_copy(d, me, s, src, dst, send, recv).wait_send()


def pack_edges(d, rows, hs, fs, tail):
    slot = lane_iota() >> 2

    @pl.loop(0, d.groups)
    def _(g):
        for q in range(d.packs):
            last = jnp.zeros((SUB, W), F32)
            lead = jnp.zeros((SUB, W), F32)
            for r in range(32 * q, min(32 * q + 32, d.rows)):
                s = r - 32 * q
                v = rows[pl.ds(pl.multiple_of(r * d.cl + g * SUB, SUB), SUB), :]
                here = slot == s
                last = jnp.where(here, pltpu.roll(v, (4 * s - (W - REACH)) % W, 1), last)
                lead = jnp.where(here, pltpu.roll(v, 4 * s, 1) if s else v, lead)
            at = pl.ds(pl.multiple_of(q * d.cl + g * SUB, SUB), SUB)
            tail[0, at, :] = last
            tail[1, at, :] = lead

    hs[...] = tail[:, : hs.shape[1], :].astype(BF16)
    north = (d.rows - REACH) * d.cl
    fs[: REACH * d.cl, :] = rows[north : north + REACH * d.cl, :].astype(BF16)


def store_shifts(x, left, right, lane, put):
    put(REACH, x)
    for k in range(1, REACH + 1):
        put(REACH - k, pltpu.roll(jnp.where(lane >= W - k, left, x), k, 1))
        put(REACH + k, pltpu.roll(jnp.where(lane < k, right, x), W - k, 1))


def build_shifts(d, rows, hr, halo, out):
    halo[:, : hr.shape[1], :] = hr[...].astype(F32)
    lane = lane_iota()

    @pl.loop(0, d.groups)
    def _(g):
        for r in range(d.rows):
            q, s = divmod(r, 32)
            at = pl.ds(pl.multiple_of(q * d.cl + g * SUB, SUB), SUB)
            left = pltpu.roll(halo[0, at, :], (W - REACH - 4 * s) % W, 1)
            right = pltpu.roll(halo[1, at, :], (W - 4 * s) % W, 1) if s else halo[1, at, :]
            x = rows[pl.ds(pl.multiple_of(r * d.cl + g * SUB, SUB), SUB), :]
            to = pl.ds(pl.multiple_of((r + REACH) * d.cl + g * SUB, SUB), SUB)

            def put(b, value, to=to):
                out[b, to, :] = value

            store_shifts(x, left, right, lane, put)


def fold_shifts(d, fr, out, base):
    count = REACH * d.cl
    flip = lax.broadcasted_iota(jnp.int32, (W, W), 0) + lax.broadcasted_iota(jnp.int32, (W, W), 1) == W - 1
    flip = flip.astype(F32).astype(BF16)
    centre, left, right = (jnp.dot(fr[j], flip, preferred_element_type=F32) for j in range(3))
    lane = lane_iota()
    for m in range(REACH):
        for g in range(d.groups):
            src = (REACH - 1 - m) * d.cl + g * SUB
            to = base + m * d.cl + g * SUB

            def put(b, value, to=to):
                out[b, to : to + SUB, :] = value

            store_shifts(centre[src : src + SUB], left[src : src + SUB], right[src : src + SUB], lane, put)


def convolve_tile(d, image, weights, tile, pad32, sub):
    base = tile * d.used
    for g in range(d.groups):
        acc = [jnp.zeros((SUB, W), F32) for _ in range(d.tile)]
        for b in range(TAPS):
            lines = [
                image[b, pl.ds(pl.multiple_of(base + t * d.cl + g * SUB, SUB), SUB), :]
                for t in range(d.tile + TAPS - 1)
            ]
            for a in range(TAPS):
                w = weights[a * TAPS + b, g * SUB : (g + 1) * SUB, :]
                acc = [acc[i] + w * lines[i + a] for i in range(d.tile)]
        for i in range(d.tile):
            pad32[i * d.cl + g * SUB : i * d.cl + (g + 1) * SUB, :] = acc[i]
    offsets = jnp.zeros((d.block - d.used, W), F32)
    for r in range(d.tile):
        here = slice(r * d.cl, (r + 1) * d.cl)
        v = pad32[here, :]
        mean = jnp.sum(v, axis=0, keepdims=True) * (1.0 / d.cl)
        high = mean.astype(BF16).astype(F32)
        low = (mean - high).astype(BF16).astype(F32)
        pad32[here, :] = v - (high + low)
        offsets = jnp.where(sub == 2 * r, high, jnp.where(sub == 2 * r + 1, low, offsets))
    pad32[d.used :, :] = offsets


def correlate(d, image, weights, out, flipped):
    blocks = d.rows // d.step

    @pl.loop(0, blocks * d.groups)
    def _(n):
        g = lax.rem(n, d.groups)
        top = n // d.groups * d.step
        acc = [jnp.zeros((SUB, W), F32) for _ in range(d.step)]
        for b in range(TAPS):
            near = TAPS - 1 - b if flipped else b
            lines = [
                image[near, pl.ds(pl.multiple_of((top + t) * d.cl + g * SUB, SUB), SUB), :]
                for t in range(d.step + TAPS - 1)
            ]
            for a in range(TAPS):
                w = weights[a * TAPS + b, pl.ds(pl.multiple_of(g * SUB, SUB), SUB), :]
                down = TAPS - 1 - a if flipped else a
                acc = [acc[i] + w * lines[i + down] for i in range(d.step)]
        for i in range(d.step):
            out[pl.ds(pl.multiple_of((top + i) * d.cl + g * SUB, SUB), SUB), :] = acc[i]


def tap_products(d, image, flat, grad):
    lane = lane_iota()
    grad[...] = jnp.zeros_like(grad)

    @pl.loop(0, TAPS * d.groups)
    def _(n):
        b = lax.rem(n, TAPS)
        g = n // TAPS
        acc = [jnp.zeros((SUB, W), F32) for _ in range(TAPS)]
        for block in range(d.rows // d.step):
            top = block * d.step
            lines = [
                image[b, pl.ds(pl.multiple_of((top + t) * d.cl + g * SUB, SUB), SUB), :]
                for t in range(d.step + TAPS - 1)
            ]
            for i in range(d.step):
                v = flat[pl.ds(pl.multiple_of((top + i) * d.cl + g * SUB, SUB), SUB), :]
                acc = [acc[a] + v * lines[i + a] for a in range(TAPS)]
        at = pl.ds(pl.multiple_of(g * SUB, SUB), SUB)
        total = grad[at, :]
        for a in range(TAPS):
            total = jnp.where(lane == a * TAPS + b, jnp.sum(acc[a], axis=1, keepdims=True), total)
        grad[at, :] = total


def column_of(vector, out):
    for j in range(vector.shape[0]):
        n = vector.shape[1]
        line = jnp.broadcast_to(vector[j : j + 1, :], (W, n))
        out[j * n : (j + 1) * n, :] = jnp.transpose(line)


def first_peer(d, lon, offset):
    z = lax.rem(lon // d.core, d.zhi)
    mine = lon // (d.core * d.zhi) * d.core + lax.rem(lon, d.core)
    theirs = lax.rem(mine + offset, d.first)
    peer = (theirs // d.core * d.zhi + z) * d.core + lax.rem(theirs, d.core)
    return mine, theirs, peer


def second_peer(d, lon, offset):
    mine = lax.rem(lon // d.core, d.zhi)
    theirs = lax.rem(mine + offset, d.zhi)
    return mine, theirs, lon + (theirs - mine) * d.core


def share_copy(d, peers, count, offset, src, dst, send, recv, arriving=False):
    mine, theirs, peer = peers(d, lax.axis_index("lon"), offset)
    return pltpu.make_async_remote_copy(
        src_ref=src, dst_ref=dst.at[theirs if arriving else mine], send_sem=send.at[theirs],
        recv_sem=recv.at[theirs if arriving else mine], device_id={"lon": peer}, device_id_type=MESH,
    )


def share_start(d, peers, count, src, dst, send, recv):
    mine, _, _ = peers(d, lax.axis_index("lon"), 1)
    for s in range(1, count):
        share_copy(d, peers, count, s, src, dst, send, recv).start()
    dst[mine] = src[...]


def share_wait(d, peers, count, src, dst, send, recv):
    for s in range(1, count):
        share_copy(d, peers, count, s, src, dst, send, recv, True).wait_recv()
    for s in range(1, count):
        share_copy(d, peers, count, s, src, dst, send, recv).wait_send()


def gather_copy(d, offset, src, dst, send, recv, arriving=False):
    me = lax.axis_index("lev")
    peer = lev_peer(d, me, offset)
    return pltpu.make_async_remote_copy(
        src_ref=src, dst_ref=dst.at[peer if arriving else me], send_sem=send.at[peer],
        recv_sem=recv.at[peer if arriving else me], device_id={"lev": peer}, device_id_type=MESH,
    )


def block_kernel(d, snap, kern, cot, mask, gain, shift, w_in_hbm, w_out_hbm, result, out, grads,
                 rows, pad32, wide, tail, shifted, weights, image, fold, sums,
                 gains, shifts, normed, rstds, lifted, upstream, projected, d_lifted, blocks, w_in, w_out,
                 grad, part1, total1, part2, total2, gathered, gflat,
                 hs, hr, fs, fr, hs2, hr2, fs2, fr2, rs, rbuf, cs, cbuf, us, ubuf, ds, dbuf,
                 w_sem, e_send, e_recv, e2_send, e2_recv, r_send, r_recv, c_send, c_recv, u_send, u_recv, d_send, d_recv,
                 p1s, p1r, p2s, p2r, gs, gr):
    lev, lon = lax.axis_index("lev"), lax.axis_index("lon")
    barrier = pltpu.get_barrier_semaphore()
    greet(d, barrier)
    for s in range(1, d.first):
        signal(barrier, {"lon": first_peer(d, lon, s)[2]})
    for s in range(1, d.zhi):
        signal(barrier, {"lon": second_peer(d, lon, s)[2]})
    w_copies = [pltpu.make_async_copy(w_in_hbm, w_in, w_sem.at[0]), pltpu.make_async_copy(w_out_hbm, w_out, w_sem.at[1])]
    for copy in w_copies:
        copy.start()
    edge = (hs, hr, fs, fr, (e_send, e_recv))
    edge2 = (hs2, hr2, fs2, fr2, (e2_send, e2_recv))
    residual = (d, rs, rbuf, r_send, r_recv)
    forward = (d, cs, cbuf, c_send, c_recv)
    upward = (d, us, ubuf, u_send, u_recv)
    backward = (d, ds, dbuf, d_send, d_recv)

    with phase("prep"):
        for c in range(d.cl):
            rows[pl.ds(c, d.rows, stride=d.cl), :] = snap[c].astype(F32)
        fs[...] = jnp.zeros_like(fs)
        fs2[...] = jnp.zeros_like(fs2)
        pack_edges(d, rows, hs, fs, tail)
        for k in range(d.levs):
            rs[k] = rows[k * d.used : (k + 1) * d.used, :].astype(BF16)
    with phase("meet"):
        met(d, barrier, d.first - 1 + d.zhi - 1)
    edge_start(d, *edge)
    blocks_start(*residual)

    with phase("weights"):
        wide[...] = jnp.zeros_like(wide)
        wide[: TAPS * TAPS, :] = kern[...].astype(F32)
        for j in range(0, d.channels, W):
            n = min(W, d.channels - j)
            gflat[j : j + n, :] = jnp.transpose(wide[:, j : j + n])
        mine = gflat[pl.ds(pl.multiple_of(lev * d.cl, SUB), d.cl), :]
        for t in range(TAPS * TAPS):
            weights[t] = jnp.broadcast_to(mine[:, t : t + 1], (d.cl, W))
        for b in range(TAPS):
            shifted[b, : REACH * d.cl, :] = jnp.zeros((REACH * d.cl, W), F32)
            image[b, : REACH * d.cl, :] = jnp.zeros((REACH * d.cl, W), F32)
            image[b, (REACH + d.rows) * d.cl :, :] = jnp.zeros((REACH * d.cl, W), F32)
        column_of(gain[...], gains)
        column_of(shift[...], shifts)
        wet = mask[...].astype(F32)
        for r in range(d.tile):
            up = cot[r].astype(F32) * wet[r : r + 1, :]
            upstream[r * W : (r + 1) * W, :] = jnp.transpose(up).astype(BF16)
            for k in range(d.levs):
                blocks[k, r * d.cl : (r + 1) * d.cl, :] = up[k * d.cl : (k + 1) * d.cl]
        for k in range(d.levs):
            us[k] = blocks[k, : d.used, :].astype(BF16)

    with phase("edge_wait"):
        edge_wait(d, *edge)
    with phase("shifts"):
        build_shifts(d, rows, hr, tail, shifted)
        fold_shifts(d, fr, shifted, (REACH + d.rows) * d.cl)

    with phase("conv"):
        sub = lax.broadcasted_iota(jnp.int32, (d.block - d.used, W), 0)

        @pl.loop(1, d.levs + 1)
        def _(s):
            peer = lev_peer(d, lev, s)
            convolve_tile(d, shifted, weights, peer, pad32, sub)
            cs[peer] = pad32[...].astype(BF16)

            @pl.when(s < d.levs)
            def _():
                block_copy(d, lev, s, cs, cbuf, c_send, c_recv).start()

        cbuf[lev] = cs[lev]

    for copy in w_copies:
        copy.wait()
    with phase("conv_wait"):
        blocks_arrive(*forward)
    blocks_start(*upward)

    with phase("norm"):
        for k in range(d.levs):
            v = cbuf[k].astype(F32)
            for r in range(d.tile):
                at = d.used + 2 * r
                normed[r, k * d.cl : (k + 1) * d.cl, :] = v[r * d.cl : (r + 1) * d.cl] + (v[at : at + 1] + v[at + 1 : at + 2])
        inv = 1.0 / d.channels
        for r in range(d.tile):
            v = normed[r]
            v = v - jnp.sum(v, axis=0, keepdims=True) * inv
            spread = jnp.sum(v * v, axis=0, keepdims=True) * inv
            rstd = lax.rsqrt(spread + epsilon)
            v = v * rstd
            normed[r] = v
            rstds[r : r + 1, :] = rstd
            lifted[r * W : (r + 1) * W, :] = jnp.transpose(v * gains[...] + shifts[...]).astype(BF16)

    with phase("mlp"):
        chunk = 256
        for n in range(d.hidden // chunk):
            f = slice(n * chunk, (n + 1) * chunk)
            hidden = jnp.dot(lifted[...], w_in[:, f], preferred_element_type=F32)
            d_active = lax.dot_general(upstream[...], w_out[f, :], (((1,), (1,)), ((), ())), preferred_element_type=F32)
            share = 0.5 * (1.0 + lax.erf(hidden * root_half))
            active = (hidden * share).astype(BF16)
            slope = share + hidden * jnp.exp(-0.5 * hidden * hidden) * inv_root_tau
            d_hidden = (d_active * slope).astype(BF16)
            p = jnp.dot(active, w_out[f, :], preferred_element_type=F32)
            q = lax.dot_general(w_in[:, f], d_hidden, (((1,), (1,)), ((), ())), preferred_element_type=F32)
            if n == 0:
                projected[...] = p
                d_lifted[...] = q
            else:
                projected[...] += p
                d_lifted[...] += q

    with phase("dconv"):
        for r in range(d.tile):
            dn = d_lifted[:, r * W : (r + 1) * W] * gains[...]
            v = normed[r]
            mean = jnp.sum(dn, axis=0, keepdims=True) * inv
            along = jnp.sum(dn * v, axis=0, keepdims=True) * inv
            normed[r] = rstds[r : r + 1, :] * (dn - mean - v * along)
            for k in range(d.levs):
                blocks[k, r * d.cl : (r + 1) * d.cl, :] = normed[r, k * d.cl : (k + 1) * d.cl, :]
        for k in range(d.levs):
            ds[k] = blocks[k, : d.used, :].astype(BF16)
    blocks_start(*backward)

    with phase("result"):
        blocks_arrive(*residual)
        for k in range(d.levs):
            blocks[k, : d.used, :] = rbuf[k].astype(F32)
        for r in range(d.tile):
            moved = jnp.transpose(projected[r * W : (r + 1) * W, :])
            for k in range(d.levs):
                part = slice(k * d.cl, (k + 1) * d.cl)
                shifts[part, :] = wet[r : r + 1, :] * (blocks[k, r * d.cl : (r + 1) * d.cl, :] + moved[part])
            result[r] = shifts[...].astype(BF16)

    with phase("d_wait"):
        blocks_arrive(*backward)
    with phase("pack2"):
        for k in range(d.levs):
            rows[k * d.used : (k + 1) * d.used, :] = dbuf[k].astype(F32)
        pack_edges(d, rows, hs2, fs2, tail)
    edge_start(d, *edge2)
    with phase("grad"):
        tap_products(d, shifted, rows, grad)
    first = (d, first_peer, d.first, grad, part1, p1s, p1r)
    share_start(*first)

    with phase("edge2_wait"):
        edge_wait(d, *edge2)
    with phase("shifts2"):
        build_shifts(d, rows, hr2, tail, image)
        fold_shifts(d, fr2, fold, 0)

    with phase("share1_wait"):
        share_wait(*first)
    total1[...] = sum(part1[i] for i in range(d.first))
    second = (d, second_peer, d.zhi, total1, part2, p2s, p2r)
    share_start(*second)

    with phase("adjoint"):
        correlate(d, image, weights, sums, True)

    with phase("share2_wait"):
        share_wait(*second)
    total2[...] = sum(part2[i] for i in range(d.zhi))
    for s in range(1, d.levs):
        gather_copy(d, s, total2, gathered, gs, gr).start()
    gathered[lev] = total2[...]

    with phase("edge_term"):
        for m in range(REACH):
            for g in range(d.groups):
                at = (d.rows - 1 - m) * d.cl + g * SUB
                acc = sums[at : at + SUB, :]
                for k in range(REACH - m):
                    for b in range(TAPS):
                        w = weights[(REACH + 1 + m + k) * TAPS + b, g * SUB : (g + 1) * SUB, :]
                        acc = acc + w * fold[b, k * d.cl + g * SUB : k * d.cl + (g + 1) * SUB, :]
                sums[at : at + SUB, :] = acc
    with phase("u_wait"):
        blocks_arrive(*upward)
    with phase("finish"):
        for k in range(d.levs):
            part = slice(k * d.used, (k + 1) * d.used)
            sums[part, :] = sums[part, :] + ubuf[k].astype(F32)
        for c in range(d.cl):
            out[c] = sums[pl.ds(c, d.rows, stride=d.cl), :].astype(BF16)

    with phase("gather_wait"):
        for s in range(1, d.levs):
            gather_copy(d, s, total2, gathered, gs, gr, True).wait_recv()
    for k in range(d.levs):
        gflat[k * d.cl : (k + 1) * d.cl, :] = gathered[k]
    for j in range(0, d.channels, W):
        n = min(W, d.channels - j)
        grads[:, j : j + n] = jnp.transpose(gflat[j : j + n, :])[: TAPS * TAPS]
    for s in range(1, d.levs):
        gather_copy(d, s, total2, gathered, gs, gr).wait_send()
    blocks_sent(*residual)
    blocks_sent(*forward)
    blocks_sent(*upward)
    blocks_sent(*backward)


VMEM = pl.BlockSpec(memory_space=pltpu.VMEM)
ANY = pl.BlockSpec(memory_space=pl.ANY)
DMA = pltpu.SemaphoreType.DMA
LIMIT = 60 * 1024 * 1024


def shards(snapshot, cotangent, ocean_mask, kernel, norm_gain, norm_shift, weight_in, weight_out):
    levs, lons = lax.axis_size("lev"), lax.axis_size("lon")
    cl, rows, _ = snapshot.shape
    d = Dims(levs, lons, cl * levs, rows, weight_in.shape[1])
    sds = jax.ShapeDtypeStruct
    f32 = lambda *shape: pltpu.VMEM(shape, F32)
    b16 = lambda *shape: pltpu.VMEM(shape, BF16)
    flat = (d.rows * d.cl, W)
    image = (TAPS, (d.rows + 2 * REACH) * d.cl, W)
    halo = (2, -(-d.packs * d.cl // 16) * 16, W)
    north = (-(-REACH * d.cl // 16) * 16, W)
    cells = d.tile * W
    share = (d.cl, W)
    result, d_snapshot, grads = pl.pallas_call(
        functools.partial(block_kernel, d),
        name="block",
        out_shape=(
            sds((d.tile, d.channels, W), BF16), sds((d.cl, d.rows, W), BF16), sds((TAPS * TAPS, d.channels), F32),
        ),
        in_specs=[VMEM] * 6 + [ANY] * 2,
        out_specs=(VMEM,) * 3,
        scratch_shapes=[
            f32(*flat), f32(d.block, W), f32(W, d.channels), f32(*halo), f32(*image), f32(TAPS * TAPS, d.cl, W),
            f32(*image), f32(TAPS, REACH * d.cl, W), f32(*flat),
            f32(d.channels, W), f32(d.channels, W), f32(d.tile, d.channels, W), f32(d.tile, W),
            b16(cells, d.channels), b16(cells, d.channels), f32(cells, d.channels), f32(d.channels, cells),
            f32(d.levs, d.block, W), b16(*weight_in.shape), b16(*weight_out.shape),
            f32(*share), f32(d.first, *share), f32(*share), f32(d.zhi, *share), f32(*share),
            f32(d.levs, *share), f32(d.channels, W),
            *[b16(*halo), b16(*halo), b16(*north), b16(3, *north)] * 2,
            b16(d.levs, d.used, W), b16(d.levs, d.used, W), b16(d.levs, d.block, W), b16(d.levs, d.block, W),
            *[b16(d.levs, d.used, W)] * 4,
            DMA((2,)), *[DMA((5,))] * 4, *[DMA((d.levs,))] * 8,
            DMA((d.first,)), DMA((d.first,)), DMA((d.zhi,)), DMA((d.zhi,)), DMA((d.levs,)), DMA((d.levs,)),
        ],
        compiler_params=pltpu.CompilerParams(collective_id=0, has_side_effects=True, vmem_limit_bytes=LIMIT),
    )(
        snapshot, kernel.T, jnp.swapaxes(cotangent, 0, 1), ocean_mask,
        norm_gain.reshape(-1, min(W, d.channels)), norm_shift.reshape(-1, min(W, d.channels)), weight_in, weight_out,
    )
    return jnp.swapaxes(result, 0, 1), d_snapshot, grads.T


def solution(mesh):
    placed = (
        P("lev", None, "lon"),
        P(None, "lev", "lon"),
        P("lev", "lon"),
        P(),
        P(),
        P(),
        P(),
        P(),
    )
    return jax.shard_map(
        shards,
        mesh=mesh,
        in_specs=placed,
        out_specs=(P(None, "lev", "lon"), P("lev", None, "lon"), P()),
        check_vma=False,
    )
```

time: 106 us -> 89.3 us (0.84); the launches traced: 106 us -> 88.3 us
  Pallas kernels: 101 us -> 83.6 us
    pallas_call x3 -> x1, Pallas kernels: 101 us -> 83.6 us  [shards(): pl.pallas_call(functools.partial(block_kernel, d), name='block', out_shap...]
    unnamed x3 -> x5, local copies, waits for them, and re-layouts: 4.91 us -> 4.06 us
where the time goes in v2:
time: 89.3 us; the launch traced here: 88.3 us
  Pallas kernels  83.6 us (94%)
  local copies, waits for them, and re-layouts  4.06 us (5%)
    pallas_call x1, Pallas kernels, shards(): pl.pallas_call(functools.partial(block_kernel, d), name='block', out_shap...  83.6 us
    unnamed x5, local copies, waits for them, and re-layouts  4.06 us

profile of v2, /device:TPU:1, one launch (start us, length us, event | category | flops | bytes accessed | tf_op | source)
XLA Modules:
  0.0 88.3 jit_solution(11027041776647389134)
XLA Ops:
  0.6 83.6 %block.1 = (bf16[3,384,128]{2,1,0:T(8,128)(2,1)}, bf16[24,48,128]{2,1,0:T(8,128)(2,1)}, f32[49,384]{1,0:T(8,128)}) custom-call(bf16[24,48,128]{2,1,0:T(8,128)(2,1)} %snap.1, bf16[49,384]{1,0:T(8,128)(2,1)} %bitcast.9, bf16[3,384,128]{2,1,0:T(8,128)(2,1)} %bitcast.6, s32[3,128]{1,0:T(4,128)} %mask.1, f32[3,128]{1,0:T(4,128)} %bitcast.10, f32[3,128]{1,0:T(4,128)} %bitcast.11, ...), custom_call_target="tpu_custom_call" | custom-call | tf_op jit(solution)/shard_map/block/pallas_call | solution.py:589
  84.3 0.0 copy-start
  84.3 1.7 %copy.14 = bf16[384,3,128]{2,0,1:T(8,128)(2,1)} copy(bf16[384,3,128]{2,0,1:T(8,128)(2,1)} %bitcast.7) | data formatting | bytes 589824
  86.0 1.7 %copy.15 = bf16[24,48,128]{2,1,0:T(8,128)(2,1)} copy(bf16[24,48,128]{2,1,0:T(8,128)(2,1)} %get-tuple-element.13) | data formatting | bytes 589824
  87.7 0.0 copy-done
  87.7 0.6 copy.16
Async XLA Ops:
  84.3 3.4 %copy-start = (f32[49,384]{1,0:T(8,128)S(1)}, f32[49,384]{1,0:T(8,128)}, u32[]{:S(2)}) copy-start(f32[49,384]{1,0:T(8,128)} %get-tuple-element.8) | copy-start | bytes 225796

commit v3 on v2

--- a/solution.py
+++ b/solution.py
@@ -37,7 +37,7 @@
         self.block = -(-(self.used + 2 * self.tile) // 16) * 16
         self.groups = self.cl // SUB
         self.step = max(r for r in (8, 6, 4, 3) if rows % r == 0)
-        self.packs = -(-rows // 32)
+        self.packs = -(-rows // 16)
         self.core = 2
         self.zhi = 4 if lons == 32 else 2
         self.x = lons // (self.core * self.zhi)
@@ -92,7 +92,7 @@
     send, recv = sems
     for j, side in enumerate(sides):
         yield None, pltpu.make_async_remote_copy(
-            src_ref=hs.at[j], dst_ref=hr.at[j], send_sem=send.at[j], recv_sem=recv.at[j],
+            src_ref=hs, dst_ref=hr.at[j], send_sem=send.at[j], recv_sem=recv.at[j],
             device_id={"lon": side}, device_id_type=MESH,
         ), None
     for j, mirror in enumerate(mirrors):
@@ -132,14 +132,15 @@
     )
 
 
-def blocks_start(d, src, dst, send, recv):
+def blocks_start(d, src, dst, send, recv, low=1, high=None):
     me = lax.axis_index("lev")
 
-    @pl.loop(1, d.levs)
+    @pl.loop(low, high or d.levs)
     def _(s):
         block_copy(d, me, s, src, dst, send, recv).start()
 
-    dst[me] = src[me]
+    if low == 1:
+        dst[me] = src[me]
 
 
 def blocks_arrive(d, src, dst, send, recv):
@@ -159,70 +160,78 @@
 
 
 def pack_edges(d, rows, hs, fs, tail):
-    slot = lane_iota() >> 2
+    slot = lane_iota() >> 3
 
     @pl.loop(0, d.groups)
     def _(g):
         for q in range(d.packs):
-            last = jnp.zeros((SUB, W), F32)
-            lead = jnp.zeros((SUB, W), F32)
-            for r in range(32 * q, min(32 * q + 32, d.rows)):
-                s = r - 32 * q
+            both = jnp.zeros((SUB, W), F32)
+            for r in range(16 * q, min(16 * q + 16, d.rows)):
+                s = r - 16 * q
                 v = rows[pl.ds(pl.multiple_of(r * d.cl + g * SUB, SUB), SUB), :]
-                here = slot == s
-                last = jnp.where(here, pltpu.roll(v, (4 * s - (W - REACH)) % W, 1), last)
-                lead = jnp.where(here, pltpu.roll(v, 4 * s, 1) if s else v, lead)
-            at = pl.ds(pl.multiple_of(q * d.cl + g * SUB, SUB), SUB)
-            tail[0, at, :] = last
-            tail[1, at, :] = lead
-
-    hs[...] = tail[:, : hs.shape[1], :].astype(BF16)
+                both = jnp.where(slot == s, pltpu.roll(v, (8 * s - (W - REACH)) % W, 1), both)
+            tail[pl.ds(pl.multiple_of(q * d.cl + g * SUB, SUB), SUB), :] = both
+
+    hs[...] = tail[...].astype(BF16)
     north = (d.rows - REACH) * d.cl
     fs[: REACH * d.cl, :] = rows[north : north + REACH * d.cl, :].astype(BF16)
 
 
-def store_shifts(x, left, right, lane, put):
-    put(REACH, x)
-    for k in range(1, REACH + 1):
-        put(REACH - k, pltpu.roll(jnp.where(lane >= W - k, left, x), k, 1))
-        put(REACH + k, pltpu.roll(jnp.where(lane < k, right, x), W - k, 1))
-
-
-def build_shifts(d, rows, hr, halo, out):
-    halo[:, : hr.shape[1], :] = hr[...].astype(F32)
-    lane = lane_iota()
+def moves():
+    row = lax.broadcasted_iota(jnp.int32, (2 * W, W), 0)
+    column = lax.broadcasted_iota(jnp.int32, (2 * W, W), 1)
+    for b in (0, 1, 2, 4, 5, 6):
+        source = column + (b - REACH)
+        yield jnp.where(row == jnp.where(source < 0, source + 2 * W, source), 1.0, 0.0).astype(BF16)
+
+
+def build_shifts(d, rows, hr, halo, padded, both, move, out):
+    west = (lax.broadcasted_iota(jnp.int32, both.shape, 1) & 7) < REACH
+    both[...] = jnp.where(west, hr[0].astype(F32), hr[1].astype(F32))
 
     @pl.loop(0, d.groups)
     def _(g):
         for r in range(d.rows):
-            q, s = divmod(r, 32)
-            at = pl.ds(pl.multiple_of(q * d.cl + g * SUB, SUB), SUB)
-            left = pltpu.roll(halo[0, at, :], (W - REACH - 4 * s) % W, 1)
-            right = pltpu.roll(halo[1, at, :], (W - 4 * s) % W, 1) if s else halo[1, at, :]
-            x = rows[pl.ds(pl.multiple_of(r * d.cl + g * SUB, SUB), SUB), :]
-            to = pl.ds(pl.multiple_of((r + REACH) * d.cl + g * SUB, SUB), SUB)
-
-            def put(b, value, to=to):
-                out[b, to, :] = value
-
-            store_shifts(x, left, right, lane, put)
-
-
-def fold_shifts(d, fr, out, base):
+            q, s = divmod(r, 16)
+            v = both[pl.ds(pl.multiple_of(q * d.cl + g * SUB, SUB), SUB), :]
+            to = pl.ds(pl.multiple_of(r * d.cl + g * SUB, SUB), SUB)
+            halo[to, :] = pltpu.roll(v, (W - REACH - 8 * s) % W, 1)
+
+    count = d.rows * d.cl
+    step = count // 3
+
+    @pl.loop(0, 3)
+    def _(n):
+        here = pl.ds(pl.multiple_of(n * step, SUB), step)
+        to = pl.ds(pl.multiple_of(REACH * d.cl + n * step, SUB), step)
+        x = rows[here, :]
+        out[REACH, to, :] = x
+        padded[:step, :W] = x.astype(BF16)
+        padded[:step, W:] = halo[here, :].astype(BF16)
+        for j in range(3):
+            moved = jnp.dot(padded[:step, :], move[:, 2 * j * W : 2 * (j + 1) * W], preferred_element_type=F32)
+            for i in range(2):
+                b = (0, 1, 2, 4, 5, 6)[2 * j + i]
+                out[b, to, :] = moved[:, i * W : (i + 1) * W]
+
+
+def fold_shifts(d, fr, padded, both, move, out, base):
     count = REACH * d.cl
     flip = lax.broadcasted_iota(jnp.int32, (W, W), 0) + lax.broadcasted_iota(jnp.int32, (W, W), 1) == W - 1
     flip = flip.astype(F32).astype(BF16)
     centre, left, right = (jnp.dot(fr[j], flip, preferred_element_type=F32) for j in range(3))
-    lane = lane_iota()
+    low = lax.broadcasted_iota(jnp.int32, (d.cl, W), 1) < W // 2
     for m in range(REACH):
-        for g in range(d.groups):
-            src = (REACH - 1 - m) * d.cl + g * SUB
-            to = base + m * d.cl + g * SUB
-
-            def put(b, value, to=to):
-                out[b, to : to + SUB, :] = value
-
-            store_shifts(centre[src : src + SUB], left[src : src + SUB], right[src : src + SUB], lane, put)
+        src = slice((REACH - 1 - m) * d.cl, (REACH - m) * d.cl)
+        out[REACH, base + m * d.cl : base + (m + 1) * d.cl, :] = centre[src]
+        both[m * d.cl : (m + 1) * d.cl, :] = jnp.where(low, right[src], left[src])
+    padded[:count, :W] = out[REACH, base : base + count, :].astype(BF16)
+    padded[:count, W:] = both[:count, :].astype(BF16)
+    for j in range(3):
+        moved = jnp.dot(padded[:count, :], move[:, 2 * j * W : 2 * (j + 1) * W], preferred_element_type=F32)
+        for i in range(2):
+            b = (0, 1, 2, 4, 5, 6)[2 * j + i]
+            out[b, base : base + count, :] = moved[:, i * W : (i + 1) * W]
 
 
 def convolve_tile(d, image, weights, tile, pad32, sub):
@@ -251,10 +260,8 @@
     pad32[d.used :, :] = offsets
 
 
-def correlate(d, image, weights, out, flipped):
-    blocks = d.rows // d.step
-
-    @pl.loop(0, blocks * d.groups)
+def correlate(d, image, weights, out, flipped, low, high):
+    @pl.loop(low, high)
     def _(n):
         g = lax.rem(n, d.groups)
         top = n // d.groups * d.step
@@ -273,28 +280,32 @@
             out[pl.ds(pl.multiple_of((top + i) * d.cl + g * SUB, SUB), SUB), :] = acc[i]
 
 
-def tap_products(d, image, flat, grad):
+def tap_tile(d, image, flat, acc, tile):
+    base = tile * d.used
+    for g in range(d.groups):
+        mine = slice(g * SUB, (g + 1) * SUB)
+        v = [flat[pl.ds(pl.multiple_of(base + i * d.cl + g * SUB, SUB), SUB), :] for i in range(d.tile)]
+        for b in range(TAPS):
+            lines = [
+                image[b, pl.ds(pl.multiple_of(base + t * d.cl + g * SUB, SUB), SUB), :]
+                for t in range(d.tile + TAPS - 1)
+            ]
+            for a in range(TAPS):
+                part = v[0] * lines[a]
+                for i in range(1, d.tile):
+                    part = part + v[i] * lines[i + a]
+                acc[a * TAPS + b, mine, :] = acc[a * TAPS + b, mine, :] + part
+
+
+def tap_totals(d, acc, grad):
     lane = lane_iota()
-    grad[...] = jnp.zeros_like(grad)
-
-    @pl.loop(0, TAPS * d.groups)
-    def _(n):
-        b = lax.rem(n, TAPS)
-        g = n // TAPS
-        acc = [jnp.zeros((SUB, W), F32) for _ in range(TAPS)]
-        for block in range(d.rows // d.step):
-            top = block * d.step
-            lines = [
-                image[b, pl.ds(pl.multiple_of((top + t) * d.cl + g * SUB, SUB), SUB), :]
-                for t in range(d.step + TAPS - 1)
-            ]
-            for i in range(d.step):
-                v = flat[pl.ds(pl.multiple_of((top + i) * d.cl + g * SUB, SUB), SUB), :]
-                acc = [acc[a] + v * lines[i + a] for a in range(TAPS)]
+
+    @pl.loop(0, d.groups)
+    def _(g):
         at = pl.ds(pl.multiple_of(g * SUB, SUB), SUB)
-        total = grad[at, :]
-        for a in range(TAPS):
-            total = jnp.where(lane == a * TAPS + b, jnp.sum(acc[a], axis=1, keepdims=True), total)
+        total = jnp.zeros((SUB, W), F32)
+        for t in range(TAPS * TAPS):
+            total = jnp.where(lane == t, jnp.sum(acc[t, at, :], axis=1, keepdims=True), total)
         grad[at, :] = total
 
 
@@ -350,10 +361,10 @@
     )
 
 
-def block_kernel(d, snap, kern, cot, mask, gain, shift, w_in_hbm, w_out_hbm, result, out, grads,
+def block_kernel(d, snap_hbm, kern, cot_hbm, mask, gain, shift, w_in_hbm, w_out_hbm, result, out, grads,
                  rows, pad32, wide, tail, shifted, weights, image, fold, sums,
                  gains, shifts, normed, rstds, lifted, upstream, projected, d_lifted, blocks, w_in, w_out,
-                 grad, part1, total1, part2, total2, gathered, gflat,
+                 grad, part1, total1, part2, total2, gathered, gflat, snap, cot, d_active, products, move, padded, halo,
                  hs, hr, fs, fr, hs2, hr2, fs2, fr2, rs, rbuf, cs, cbuf, us, ubuf, ds, dbuf,
                  w_sem, e_send, e_recv, e2_send, e2_recv, r_send, r_recv, c_send, c_recv, u_send, u_recv, d_send, d_recv,
                  p1s, p1r, p2s, p2r, gs, gr):
@@ -364,6 +375,10 @@
         signal(barrier, {"lon": first_peer(d, lon, s)[2]})
     for s in range(1, d.zhi):
         signal(barrier, {"lon": second_peer(d, lon, s)[2]})
+    snap_copy = pltpu.make_async_copy(snap_hbm, snap, w_sem.at[2])
+    snap_copy.start()
+    cot_copy = pltpu.make_async_copy(cot_hbm, cot, w_sem.at[3])
+    cot_copy.start()
     w_copies = [pltpu.make_async_copy(w_in_hbm, w_in, w_sem.at[0]), pltpu.make_async_copy(w_out_hbm, w_out, w_sem.at[1])]
     for copy in w_copies:
         copy.start()
@@ -375,8 +390,10 @@
     backward = (d, ds, dbuf, d_send, d_recv)
 
     with phase("prep"):
+        snap_copy.wait()
         for c in range(d.cl):
             rows[pl.ds(c, d.rows, stride=d.cl), :] = snap[c].astype(F32)
+        tail[...] = jnp.zeros_like(tail)
         fs[...] = jnp.zeros_like(fs)
         fs2[...] = jnp.zeros_like(fs2)
         pack_edges(d, rows, hs, fs, tail)
@@ -385,9 +402,12 @@
     with phase("meet"):
         met(d, barrier, d.first - 1 + d.zhi - 1)
     edge_start(d, *edge)
-    blocks_start(*residual)
+    early = d.levs // 2
+    blocks_start(*residual, 1, early)
 
     with phase("weights"):
+        for j, m in enumerate(moves()):
+            move[:, j * W : (j + 1) * W] = m
         wide[...] = jnp.zeros_like(wide)
         wide[: TAPS * TAPS, :] = kern[...].astype(F32)
         for j in range(0, d.channels, W):
@@ -400,6 +420,32 @@
             shifted[b, : REACH * d.cl, :] = jnp.zeros((REACH * d.cl, W), F32)
             image[b, : REACH * d.cl, :] = jnp.zeros((REACH * d.cl, W), F32)
             image[b, (REACH + d.rows) * d.cl :, :] = jnp.zeros((REACH * d.cl, W), F32)
+
+    with phase("edge_wait"):
+        edge_wait(d, *edge)
+    with phase("shifts"):
+        build_shifts(d, rows, hr, halo, padded, tail, move, shifted)
+        fold_shifts(d, fr, padded, tail, move, shifted, (REACH + d.rows) * d.cl)
+
+    with phase("conv"):
+        sub = lax.broadcasted_iota(jnp.int32, (d.block - d.used, W), 0)
+
+        @pl.loop(1, d.levs + 1)
+        def _(s):
+            peer = lev_peer(d, lev, s)
+            convolve_tile(d, shifted, weights, peer, pad32, sub)
+            cs[peer] = pad32[...].astype(BF16)
+
+            @pl.when(s < d.levs)
+            def _():
+                block_copy(d, lev, s, cs, cbuf, c_send, c_recv).start()
+
+        cbuf[lev] = cs[lev]
+
+    chunk = 256
+    chunks = [slice(n, n + chunk) for n in range(0, d.hidden, chunk)]
+    with phase("upstream"):
+        cot_copy.wait()
         column_of(gain[...], gains)
         column_of(shift[...], shifts)
         wet = mask[...].astype(F32)
@@ -410,33 +456,15 @@
                 blocks[k, r * d.cl : (r + 1) * d.cl, :] = up[k * d.cl : (k + 1) * d.cl]
         for k in range(d.levs):
             us[k] = blocks[k, : d.used, :].astype(BF16)
-
-    with phase("edge_wait"):
-        edge_wait(d, *edge)
-    with phase("shifts"):
-        build_shifts(d, rows, hr, tail, shifted)
-        fold_shifts(d, fr, shifted, (REACH + d.rows) * d.cl)
-
-    with phase("conv"):
-        sub = lax.broadcasted_iota(jnp.int32, (d.block - d.used, W), 0)
-
-        @pl.loop(1, d.levs + 1)
-        def _(s):
-            peer = lev_peer(d, lev, s)
-            convolve_tile(d, shifted, weights, peer, pad32, sub)
-            cs[peer] = pad32[...].astype(BF16)
-
-            @pl.when(s < d.levs)
-            def _():
-                block_copy(d, lev, s, cs, cbuf, c_send, c_recv).start()
-
-        cbuf[lev] = cs[lev]
-
-    for copy in w_copies:
-        copy.wait()
+        for copy in w_copies:
+            copy.wait()
+        for f in chunks:
+            d_active[:, f] = lax.dot_general(
+                upstream[...], w_out[f, :], (((1,), (1,)), ((), ())), preferred_element_type=F32
+            )
     with phase("conv_wait"):
         blocks_arrive(*forward)
-    blocks_start(*upward)
+    blocks_start(*residual, early)
 
     with phase("norm"):
         for k in range(d.levs):
@@ -456,15 +484,12 @@
             lifted[r * W : (r + 1) * W, :] = jnp.transpose(v * gains[...] + shifts[...]).astype(BF16)
 
     with phase("mlp"):
-        chunk = 256
-        for n in range(d.hidden // chunk):
-            f = slice(n * chunk, (n + 1) * chunk)
+        for n, f in enumerate(chunks):
             hidden = jnp.dot(lifted[...], w_in[:, f], preferred_element_type=F32)
-            d_active = lax.dot_general(upstream[...], w_out[f, :], (((1,), (1,)), ((), ())), preferred_element_type=F32)
             share = 0.5 * (1.0 + lax.erf(hidden * root_half))
             active = (hidden * share).astype(BF16)
             slope = share + hidden * jnp.exp(-0.5 * hidden * hidden) * inv_root_tau
-            d_hidden = (d_active * slope).astype(BF16)
+            d_hidden = (d_active[:, f] * slope).astype(BF16)
             p = jnp.dot(active, w_out[f, :], preferred_element_type=F32)
             q = lax.dot_general(w_in[:, f], d_hidden, (((1,), (1,)), ((), ())), preferred_element_type=F32)
             if n == 0:
@@ -487,6 +512,28 @@
             ds[k] = blocks[k, : d.used, :].astype(BF16)
     blocks_start(*backward)
 
+    blocks_start(*upward)
+    products[...] = jnp.zeros_like(products)
+    with phase("grad"):
+
+        @pl.loop(0, d.levs)
+        def _(s):
+            tile = lev_peer(d, lev, d.levs - s)
+
+            @pl.when(s > 0)
+            def _():
+                block_copy(d, lev, d.levs - s, ds, dbuf, d_send, d_recv, True).wait_recv()
+
+            rows[pl.ds(pl.multiple_of(tile * d.used, SUB), d.used), :] = dbuf[tile].astype(F32)
+            tap_tile(d, shifted, rows, products, tile)
+
+    with phase("pack2"):
+        pack_edges(d, rows, hs2, fs2, tail)
+    edge_start(d, *edge2)
+    tap_totals(d, products, grad)
+    first = (d, first_peer, d.first, grad, part1, p1s, p1r)
+    share_start(*first)
+
     with phase("result"):
         blocks_arrive(*residual)
         for k in range(d.levs):
@@ -498,32 +545,22 @@
                 shifts[part, :] = wet[r : r + 1, :] * (blocks[k, r * d.cl : (r + 1) * d.cl, :] + moved[part])
             result[r] = shifts[...].astype(BF16)
 
-    with phase("d_wait"):
-        blocks_arrive(*backward)
-    with phase("pack2"):
-        for k in range(d.levs):
-            rows[k * d.used : (k + 1) * d.used, :] = dbuf[k].astype(F32)
-        pack_edges(d, rows, hs2, fs2, tail)
-    edge_start(d, *edge2)
-    with phase("grad"):
-        tap_products(d, shifted, rows, grad)
-    first = (d, first_peer, d.first, grad, part1, p1s, p1r)
-    share_start(*first)
-
-    with phase("edge2_wait"):
-        edge_wait(d, *edge2)
-    with phase("shifts2"):
-        build_shifts(d, rows, hr2, tail, image)
-        fold_shifts(d, fr2, fold, 0)
-
     with phase("share1_wait"):
         share_wait(*first)
     total1[...] = sum(part1[i] for i in range(d.first))
     second = (d, second_peer, d.zhi, total1, part2, p2s, p2r)
     share_start(*second)
 
+    with phase("edge2_wait"):
+        edge_wait(d, *edge2)
+    with phase("shifts2"):
+        build_shifts(d, rows, hr2, halo, padded, tail, move, image)
+        fold_shifts(d, fr2, padded, tail, move, fold, 0)
+
     with phase("adjoint"):
-        correlate(d, image, weights, sums, True)
+        steps = d.rows // d.step * d.groups
+        half = steps // 2
+        correlate(d, image, weights, sums, True, 0, half)
 
     with phase("share2_wait"):
         share_wait(*second)
@@ -532,6 +569,8 @@
         gather_copy(d, s, total2, gathered, gs, gr).start()
     gathered[lev] = total2[...]
 
+    with phase("adjoint2"):
+        correlate(d, image, weights, sums, True, half, steps)
     with phase("edge_term"):
         for m in range(REACH):
             for g in range(d.groups):
@@ -567,6 +606,11 @@
     blocks_sent(*backward)
 
 
+def settle(*refs):
+    for source, target in zip(refs[:3], refs[3:]):
+        target[...] = source[...]
+
+
 VMEM = pl.BlockSpec(memory_space=pltpu.VMEM)
 ANY = pl.BlockSpec(memory_space=pl.ANY)
 DMA = pltpu.SemaphoreType.DMA
@@ -582,7 +626,7 @@
     b16 = lambda *shape: pltpu.VMEM(shape, BF16)
     flat = (d.rows * d.cl, W)
     image = (TAPS, (d.rows + 2 * REACH) * d.cl, W)
-    halo = (2, -(-d.packs * d.cl // 16) * 16, W)
+    halo = (-(-max(d.packs, REACH) * d.cl // 16) * 16, W)
     north = (-(-REACH * d.cl // 16) * 16, W)
     cells = d.tile * W
     share = (d.cl, W)
@@ -592,7 +636,7 @@
         out_shape=(
             sds((d.tile, d.channels, W), BF16), sds((d.cl, d.rows, W), BF16), sds((TAPS * TAPS, d.channels), F32),
         ),
-        in_specs=[VMEM] * 6 + [ANY] * 2,
+        in_specs=[ANY, VMEM, ANY, VMEM, VMEM, VMEM, ANY, ANY],
         out_specs=(VMEM,) * 3,
         scratch_shapes=[
             f32(*flat), f32(d.block, W), f32(W, d.channels), f32(*halo), f32(*image), f32(TAPS * TAPS, d.cl, W),
@@ -601,11 +645,13 @@
             b16(cells, d.channels), b16(cells, d.channels), f32(cells, d.channels), f32(d.channels, cells),
             f32(d.levs, d.block, W), b16(*weight_in.shape), b16(*weight_out.shape),
             f32(*share), f32(d.first, *share), f32(*share), f32(d.zhi, *share), f32(*share),
-            f32(d.levs, *share), f32(d.channels, W),
-            *[b16(*halo), b16(*halo), b16(*north), b16(3, *north)] * 2,
+            f32(d.levs, *share), f32(d.channels, W), b16(d.cl, d.rows, W), b16(d.tile, d.channels, W),
+            f32(cells, d.hidden), f32(TAPS * TAPS, d.cl, W),
+            b16(2 * W, 6 * W), b16(max(d.rows * d.cl // 3, REACH * d.cl), 2 * W), f32(*flat),
+            *[b16(*halo), b16(2, *halo), b16(*north), b16(3, *north)] * 2,
             b16(d.levs, d.used, W), b16(d.levs, d.used, W), b16(d.levs, d.block, W), b16(d.levs, d.block, W),
             *[b16(d.levs, d.used, W)] * 4,
-            DMA((2,)), *[DMA((5,))] * 4, *[DMA((d.levs,))] * 8,
+            DMA((4,)), *[DMA((5,))] * 4, *[DMA((d.levs,))] * 8,
             DMA((d.first,)), DMA((d.first,)), DMA((d.zhi,)), DMA((d.zhi,)), DMA((d.levs,)), DMA((d.levs,)),
         ],
         compiler_params=pltpu.CompilerParams(collective_id=0, has_side_effects=True, vmem_limit_bytes=LIMIT),
@@ -613,6 +659,13 @@
         snapshot, kernel.T, jnp.swapaxes(cotangent, 0, 1), ocean_mask,
         norm_gain.reshape(-1, min(W, d.channels)), norm_shift.reshape(-1, min(W, d.channels)), weight_in, weight_out,
     )
+    result, d_snapshot, grads = pl.pallas_call(
+        settle,
+        name="settle",
+        out_shape=tuple(sds(x.shape, x.dtype) for x in (result, d_snapshot, grads)),
+        in_specs=[VMEM] * 3,
+        out_specs=(VMEM,) * 3,
+    )(result, d_snapshot, grads)
     return jnp.swapaxes(result, 0, 1), d_snapshot, grads.T
 
 

time: 89.3 us -> 71.7 us (0.80)
  Pallas kernels: 83.6 us -> 70 us
  local copies, waits for them, and re-layouts: 4.06 us -> 0 us
    pallas_call x1, Pallas kernels: 83.6 us -> 68.1 us  [shards(): pl.pallas_call(functools.partial(block_kernel, d), name='block', out_shap...]
    unnamed x5 -> x0, local copies, waits for them, and re-layouts: 4.06 us -> none
    pallas_call x0 -> x1, Pallas kernels: none -> 1.92 us  [shards(): pl.pallas_call(settle, name='settle', out_shape=tuple((sds(x.shape, x.dty...]
where the time goes in v3:
time: 71.7 us; the launch traced here: 70.7 us
  Pallas kernels  70 us (98%)
    pallas_call x1, Pallas kernels, shards(): pl.pallas_call(functools.partial(block_kernel, d), name='block', out_shap...  68.1 us
    pallas_call x1, Pallas kernels, shards(): pl.pallas_call(settle, name='settle', out_shape=tuple((sds(x.shape, x.dty...  1.92 us

profile of v3, /device:TPU:1, one launch (start us, length us, event | category | flops | bytes accessed | tf_op | source)
XLA Modules:
  0.0 70.7 jit_solution(14762100373760382536)
XLA Ops:
  0.6 68.1 %block.1 = (bf16[3,384,128]{2,1,0:T(8,128)(2,1)}, bf16[24,48,128]{2,1,0:T(8,128)(2,1)}, f32[49,384]{1,0:T(8,128)}) custom-call(bf16[24,48,128]{2,1,0:T(8,128)(2,1)} %snap_hbm.1, bf16[49,384]{1,0:T(8,128)(2,1)} %bitcast.7, bf16[3,384,128]{2,1,0:T(8,128)(2,1)} %bitcast.6, s32[3,128]{1,0:T(4,128)} %mask.1, f32[3,128]{1,0:T(4,128)} %bitcast.8, ...), custom_call_target="tpu_custom_call" | custom-call | tf_op jit(solution)/shard_map/block/pallas_call | solution.py:633
  68.7 1.9 %settle.1 = (bf16[3,384,128]{2,1,0:T(8,128)(2,1)}, bf16[24,48,128]{2,1,0:T(8,128)(2,1)}, f32[49,384]{1,0:T(8,128)}) custom-call(bf16[3,384,128]{2,1,0:T(8,128)(2,1)} %get-tuple-element.9.refs_0_, bf16[24,48,128]{2,1,0:T(8,128)(2,1)} %get-tuple-element.10.refs_1_, f32[49,384]{1,0:T(8,128)} %get-tuple-element.11.refs_2_), custom_call_target="tpu_custom_call" | custom-call | tf_op jit(solution)/shard_map/settle/pallas_call | solution.py:662

commit v4 on v3

--- a/solution.py
+++ b/solution.py
@@ -33,8 +33,9 @@
         self.levs, self.lons, self.channels, self.rows, self.hidden = levs, lons, channels, rows, hidden
         self.cl = channels // levs
         self.tile = rows // levs
+        self.room = -(-(self.cl + 2) // 8) * 8
+        self.quad = 4
         self.used = self.tile * self.cl
-        self.block = -(-(self.used + 2 * self.tile) // 16) * 16
         self.groups = self.cl // SUB
         self.step = max(r for r in (8, 6, 4, 3) if rows % r == 0)
         self.packs = -(-rows // 16)
@@ -175,6 +176,18 @@
     hs[...] = tail[...].astype(BF16)
     north = (d.rows - REACH) * d.cl
     fs[: REACH * d.cl, :] = rows[north : north + REACH * d.cl, :].astype(BF16)
+
+
+def pack_tile(d, rows, tail, tile):
+    slot = lane_iota() >> 3
+    for i in range(d.tile):
+        r = tile * d.tile + i
+        s = lax.rem(r, 16)
+        turn = lax.rem(8 * s + REACH, W)
+        for g in range(d.groups):
+            v = rows[pl.ds(pl.multiple_of(r * d.cl + g * SUB, SUB), SUB), :]
+            at = pl.ds(pl.multiple_of(r // 16 * d.cl + g * SUB, SUB), SUB)
+            tail[at, :] = jnp.where(slot == s, pltpu.roll(v, turn, 1), tail[at, :])
 
 
 def moves():
@@ -234,30 +247,55 @@
             out[b, base : base + count, :] = moved[:, i * W : (i + 1) * W]
 
 
-def convolve_tile(d, image, weights, tile, pad32, sub):
-    base = tile * d.used
+def convolve_rows(d, image, weights, r, first, pad32, sub):
+    base = (first * d.tile + r) * d.cl
     for g in range(d.groups):
-        acc = [jnp.zeros((SUB, W), F32) for _ in range(d.tile)]
+        acc = [jnp.zeros((SUB, W), F32) for _ in range(d.quad)]
         for b in range(TAPS):
             lines = [
                 image[b, pl.ds(pl.multiple_of(base + t * d.cl + g * SUB, SUB), SUB), :]
-                for t in range(d.tile + TAPS - 1)
+                for t in range((d.quad - 1) * d.tile + TAPS)
             ]
             for a in range(TAPS):
                 w = weights[a * TAPS + b, g * SUB : (g + 1) * SUB, :]
-                acc = [acc[i] + w * lines[i + a] for i in range(d.tile)]
-        for i in range(d.tile):
-            pad32[i * d.cl + g * SUB : i * d.cl + (g + 1) * SUB, :] = acc[i]
-    offsets = jnp.zeros((d.block - d.used, W), F32)
-    for r in range(d.tile):
-        here = slice(r * d.cl, (r + 1) * d.cl)
-        v = pad32[here, :]
+                acc = [acc[k] + w * lines[k * d.tile + a] for k in range(d.quad)]
+        for k in range(d.quad):
+            pad32[k, g * SUB : (g + 1) * SUB, :] = acc[k]
+    for k in range(d.quad):
+        v = pad32[k, : d.cl, :]
         mean = jnp.sum(v, axis=0, keepdims=True) * (1.0 / d.cl)
         high = mean.astype(BF16).astype(F32)
         low = (mean - high).astype(BF16).astype(F32)
-        pad32[here, :] = v - (high + low)
-        offsets = jnp.where(sub == 2 * r, high, jnp.where(sub == 2 * r + 1, low, offsets))
-    pad32[d.used :, :] = offsets
+        pad32[k, : d.cl, :] = v - (high + low)
+        pad32[k, d.cl :, :] = jnp.where(sub == 0, high, jnp.where(sub == 1, low, 0.0))
+
+
+def row_copy(d, me, peer, r, src, dst, send, recv, arriving=False):
+    return pltpu.make_async_remote_copy(
+        src_ref=src.at[r, peer],
+        dst_ref=dst.at[r, peer if arriving else me],
+        send_sem=send.at[r, peer],
+        recv_sem=recv.at[r, peer if arriving else me],
+        device_id={"lev": peer},
+        device_id_type=MESH,
+    )
+
+
+def rows_arrive(d, r, *refs):
+    me = lax.axis_index("lev")
+
+    @pl.loop(1, d.levs)
+    def _(s):
+        row_copy(d, me, lev_peer(d, me, s), r, *refs, True).wait_recv()
+
+
+def rows_sent(d, *refs):
+    me = lax.axis_index("lev")
+    for r in range(d.tile):
+
+        @pl.loop(1, d.levs)
+        def _(s):
+            row_copy(d, me, lev_peer(d, me, s), r, *refs).wait_send()
 
 
 def correlate(d, image, weights, out, flipped, low, high):
@@ -385,9 +423,9 @@
     edge = (hs, hr, fs, fr, (e_send, e_recv))
     edge2 = (hs2, hr2, fs2, fr2, (e2_send, e2_recv))
     residual = (d, rs, rbuf, r_send, r_recv)
-    forward = (d, cs, cbuf, c_send, c_recv)
+    forward = (cs, cbuf, c_send, c_recv)
     upward = (d, us, ubuf, u_send, u_recv)
-    backward = (d, ds, dbuf, d_send, d_recv)
+    backward = (ds, dbuf, d_send, d_recv)
 
     with phase("prep"):
         snap_copy.wait()
@@ -402,8 +440,7 @@
     with phase("meet"):
         met(d, barrier, d.first - 1 + d.zhi - 1)
     edge_start(d, *edge)
-    early = d.levs // 2
-    blocks_start(*residual, 1, early)
+    blocks_start(*residual)
 
     with phase("weights"):
         for j, m in enumerate(moves()):
@@ -428,19 +465,23 @@
         fold_shifts(d, fr, padded, tail, move, shifted, (REACH + d.rows) * d.cl)
 
     with phase("conv"):
-        sub = lax.broadcasted_iota(jnp.int32, (d.block - d.used, W), 0)
-
-        @pl.loop(1, d.levs + 1)
-        def _(s):
-            peer = lev_peer(d, lev, s)
-            convolve_tile(d, shifted, weights, peer, pad32, sub)
-            cs[peer] = pad32[...].astype(BF16)
-
-            @pl.when(s < d.levs)
-            def _():
-                block_copy(d, lev, s, cs, cbuf, c_send, c_recv).start()
-
-        cbuf[lev] = cs[lev]
+        sub = lax.broadcasted_iota(jnp.int32, (d.room - d.cl, W), 0)
+        parts = d.levs // d.quad
+
+        @pl.loop(0, d.tile * parts)
+        def _(n):
+            r = n // parts
+            tile = lax.rem(lev // d.quad + n, parts) * d.quad
+            convolve_rows(d, shifted, weights, r, tile, pad32, sub)
+            for k in range(d.quad):
+                cs[r, tile + k] = pad32[k].astype(BF16)
+
+                @pl.when(tile + k != lev)
+                def _():
+                    row_copy(d, lev, tile + k, r, *forward).start()
+
+        for r in range(d.tile):
+            cbuf[r, lev] = cs[r, lev]
 
     chunk = 256
     chunks = [slice(n, n + chunk) for n in range(0, d.hidden, chunk)]
@@ -455,25 +496,22 @@
             for k in range(d.levs):
                 blocks[k, r * d.cl : (r + 1) * d.cl, :] = up[k * d.cl : (k + 1) * d.cl]
         for k in range(d.levs):
-            us[k] = blocks[k, : d.used, :].astype(BF16)
+            us[k] = blocks[k].astype(BF16)
         for copy in w_copies:
             copy.wait()
         for f in chunks:
             d_active[:, f] = lax.dot_general(
                 upstream[...], w_out[f, :], (((1,), (1,)), ((), ())), preferred_element_type=F32
             )
-    with phase("conv_wait"):
-        blocks_arrive(*forward)
-    blocks_start(*residual, early)
-
-    with phase("norm"):
-        for k in range(d.levs):
-            v = cbuf[k].astype(F32)
-            for r in range(d.tile):
-                at = d.used + 2 * r
-                normed[r, k * d.cl : (k + 1) * d.cl, :] = v[r * d.cl : (r + 1) * d.cl] + (v[at : at + 1] + v[at + 1 : at + 2])
-        inv = 1.0 / d.channels
-        for r in range(d.tile):
+    inv = 1.0 / d.channels
+    for r in range(d.tile):
+        cells = slice(r * W, (r + 1) * W)
+        with phase("conv_wait"):
+            rows_arrive(d, r, *forward)
+        with phase("norm"):
+            for k in range(d.levs):
+                v = cbuf[r, k].astype(F32)
+                normed[r, k * d.cl : (k + 1) * d.cl, :] = v[: d.cl] + (v[d.cl : d.cl + 1] + v[d.cl + 1 : d.cl + 2])
             v = normed[r]
             v = v - jnp.sum(v, axis=0, keepdims=True) * inv
             spread = jnp.sum(v * v, axis=0, keepdims=True) * inv
@@ -481,36 +519,36 @@
             v = v * rstd
             normed[r] = v
             rstds[r : r + 1, :] = rstd
-            lifted[r * W : (r + 1) * W, :] = jnp.transpose(v * gains[...] + shifts[...]).astype(BF16)
-
-    with phase("mlp"):
-        for n, f in enumerate(chunks):
-            hidden = jnp.dot(lifted[...], w_in[:, f], preferred_element_type=F32)
-            share = 0.5 * (1.0 + lax.erf(hidden * root_half))
-            active = (hidden * share).astype(BF16)
-            slope = share + hidden * jnp.exp(-0.5 * hidden * hidden) * inv_root_tau
-            d_hidden = (d_active[:, f] * slope).astype(BF16)
-            p = jnp.dot(active, w_out[f, :], preferred_element_type=F32)
-            q = lax.dot_general(w_in[:, f], d_hidden, (((1,), (1,)), ((), ())), preferred_element_type=F32)
-            if n == 0:
-                projected[...] = p
-                d_lifted[...] = q
-            else:
-                projected[...] += p
-                d_lifted[...] += q
-
-    with phase("dconv"):
-        for r in range(d.tile):
-            dn = d_lifted[:, r * W : (r + 1) * W] * gains[...]
+            lifted[cells, :] = jnp.transpose(v * gains[...] + shifts[...]).astype(BF16)
+        with phase("mlp"):
+            for n, f in enumerate(chunks):
+                hidden = jnp.dot(lifted[cells, :], w_in[:, f], preferred_element_type=F32)
+                share = 0.5 * (1.0 + lax.erf(hidden * root_half))
+                active = (hidden * share).astype(BF16)
+                slope = share + hidden * jnp.exp(-0.5 * hidden * hidden) * inv_root_tau
+                d_hidden = (d_active[cells, f] * slope).astype(BF16)
+                p = jnp.dot(active, w_out[f, :], preferred_element_type=F32)
+                q = lax.dot_general(w_in[:, f], d_hidden, (((1,), (1,)), ((), ())), preferred_element_type=F32)
+                if n == 0:
+                    projected[cells, :] = p
+                    d_lifted[:, cells] = q
+                else:
+                    projected[cells, :] += p
+                    d_lifted[:, cells] += q
+        with phase("dconv"):
+            dn = d_lifted[:, cells] * gains[...]
             v = normed[r]
             mean = jnp.sum(dn, axis=0, keepdims=True) * inv
             along = jnp.sum(dn * v, axis=0, keepdims=True) * inv
             normed[r] = rstds[r : r + 1, :] * (dn - mean - v * along)
             for k in range(d.levs):
-                blocks[k, r * d.cl : (r + 1) * d.cl, :] = normed[r, k * d.cl : (k + 1) * d.cl, :]
-        for k in range(d.levs):
-            ds[k] = blocks[k, : d.used, :].astype(BF16)
-    blocks_start(*backward)
+                ds[r, k] = normed[r, k * d.cl : (k + 1) * d.cl, :].astype(BF16)
+
+        @pl.loop(1, d.levs)
+        def _(s):
+            row_copy(d, lev, lev_peer(d, lev, s), r, *backward).start()
+
+        dbuf[r, lev] = ds[r, lev]
 
     blocks_start(*upward)
     products[...] = jnp.zeros_like(products)
@@ -522,13 +560,19 @@
 
             @pl.when(s > 0)
             def _():
-                block_copy(d, lev, d.levs - s, ds, dbuf, d_send, d_recv, True).wait_recv()
-
-            rows[pl.ds(pl.multiple_of(tile * d.used, SUB), d.used), :] = dbuf[tile].astype(F32)
+                for r in range(d.tile):
+                    row_copy(d, lev, tile, r, *backward, True).wait_recv()
+
+            for r in range(d.tile):
+                at = pl.ds(pl.multiple_of(tile * d.used + r * d.cl, SUB), d.cl)
+                rows[at, :] = dbuf[r, tile].astype(F32)
             tap_tile(d, shifted, rows, products, tile)
+            pack_tile(d, rows, tail, tile)
 
     with phase("pack2"):
-        pack_edges(d, rows, hs2, fs2, tail)
+        hs2[...] = tail[...].astype(BF16)
+        north = (d.rows - REACH) * d.cl
+        fs2[: REACH * d.cl, :] = rows[north : north + REACH * d.cl, :].astype(BF16)
     edge_start(d, *edge2)
     tap_totals(d, products, grad)
     first = (d, first_peer, d.first, grad, part1, p1s, p1r)
@@ -537,7 +581,7 @@
     with phase("result"):
         blocks_arrive(*residual)
         for k in range(d.levs):
-            blocks[k, : d.used, :] = rbuf[k].astype(F32)
+            blocks[k] = rbuf[k].astype(F32)
         for r in range(d.tile):
             moved = jnp.transpose(projected[r * W : (r + 1) * W, :])
             for k in range(d.levs):
@@ -601,9 +645,9 @@
     for s in range(1, d.levs):
         gather_copy(d, s, total2, gathered, gs, gr).wait_send()
     blocks_sent(*residual)
-    blocks_sent(*forward)
+    rows_sent(d, *forward)
     blocks_sent(*upward)
-    blocks_sent(*backward)
+    rows_sent(d, *backward)
 
 
 def settle(*refs):
@@ -639,19 +683,22 @@
         in_specs=[ANY, VMEM, ANY, VMEM, VMEM, VMEM, ANY, ANY],
         out_specs=(VMEM,) * 3,
         scratch_shapes=[
-            f32(*flat), f32(d.block, W), f32(W, d.channels), f32(*halo), f32(*image), f32(TAPS * TAPS, d.cl, W),
+            f32(*flat), f32(d.quad, d.room, W), f32(W, d.channels), f32(*halo), f32(*image), f32(TAPS * TAPS, d.cl, W),
             f32(*image), f32(TAPS, REACH * d.cl, W), f32(*flat),
             f32(d.channels, W), f32(d.channels, W), f32(d.tile, d.channels, W), f32(d.tile, W),
             b16(cells, d.channels), b16(cells, d.channels), f32(cells, d.channels), f32(d.channels, cells),
-            f32(d.levs, d.block, W), b16(*weight_in.shape), b16(*weight_out.shape),
+            f32(d.levs, d.used, W), b16(*weight_in.shape), b16(*weight_out.shape),
             f32(*share), f32(d.first, *share), f32(*share), f32(d.zhi, *share), f32(*share),
             f32(d.levs, *share), f32(d.channels, W), b16(d.cl, d.rows, W), b16(d.tile, d.channels, W),
             f32(cells, d.hidden), f32(TAPS * TAPS, d.cl, W),
             b16(2 * W, 6 * W), b16(max(d.rows * d.cl // 3, REACH * d.cl), 2 * W), f32(*flat),
             *[b16(*halo), b16(2, *halo), b16(*north), b16(3, *north)] * 2,
-            b16(d.levs, d.used, W), b16(d.levs, d.used, W), b16(d.levs, d.block, W), b16(d.levs, d.block, W),
-            *[b16(d.levs, d.used, W)] * 4,
-            DMA((4,)), *[DMA((5,))] * 4, *[DMA((d.levs,))] * 8,
+            b16(d.levs, d.used, W), b16(d.levs, d.used, W),
+            *[b16(d.tile, d.levs, d.room, W)] * 2,
+            b16(d.levs, d.used, W), b16(d.levs, d.used, W),
+            *[b16(d.tile, d.levs, d.cl, W)] * 2,
+            DMA((4,)), *[DMA((5,))] * 4, DMA((d.levs,)), DMA((d.levs,)), DMA((d.tile, d.levs)), DMA((d.tile, d.levs)),
+            DMA((d.levs,)), DMA((d.levs,)), DMA((d.tile, d.levs)), DMA((d.tile, d.levs)),
             DMA((d.first,)), DMA((d.first,)), DMA((d.zhi,)), DMA((d.zhi,)), DMA((d.levs,)), DMA((d.levs,)),
         ],
         compiler_params=pltpu.CompilerParams(collective_id=0, has_side_effects=True, vmem_limit_bytes=LIMIT),

time: 71.7 us -> 70.4 us (0.982); the launches traced: 70.7 us -> 70.2 us
  no operation moved by 1% of the time
where the time goes in v4:
time: 70.4 us; the launch traced here: 70.2 us
  Pallas kernels  69.6 us (99%)
    pallas_call x1, Pallas kernels, shards(): pl.pallas_call(functools.partial(block_kernel, d), name='block', out_shap...  67.7 us
    pallas_call x1, Pallas kernels, shards(): pl.pallas_call(settle, name='settle', out_shape=tuple((sds(x.shape, x.dty...  1.92 us

profile of v4, /device:TPU:1, one launch (start us, length us, event | category | flops | bytes accessed | tf_op | source)
XLA Modules:
  0.0 70.2 jit_solution(16320227855833672157)
XLA Ops:
  0.6 67.7 %block.1 = (bf16[3,384,128]{2,1,0:T(8,128)(2,1)}, bf16[24,48,128]{2,1,0:T(8,128)(2,1)}, f32[49,384]{1,0:T(8,128)}) custom-call(bf16[24,48,128]{2,1,0:T(8,128)(2,1)} %snap_hbm.1, bf16[49,384]{1,0:T(8,128)(2,1)} %bitcast.7, bf16[3,384,128]{2,1,0:T(8,128)(2,1)} %bitcast.6, s32[3,128]{1,0:T(4,128)} %mask.1, f32[3,128]{1,0:T(4,128)} %bitcast.8, ...), custom_call_target="tpu_custom_call" | custom-call | tf_op jit(solution)/shard_map/block/pallas_call | solution.py:677
  68.3 1.9 %settle.1 = (bf16[3,384,128]{2,1,0:T(8,128)(2,1)}, bf16[24,48,128]{2,1,0:T(8,128)(2,1)}, f32[49,384]{1,0:T(8,128)}) custom-call(bf16[3,384,128]{2,1,0:T(8,128)(2,1)} %get-tuple-element.9.refs_0_, bf16[24,48,128]{2,1,0:T(8,128)(2,1)} %get-tuple-element.10.refs_1_, f32[49,384]{1,0:T(8,128)} %get-tuple-element.11.refs_2_), custom_call_target="tpu_custom_call" | custom-call | tf_op jit(solution)/shard_map/settle/pallas_call | solution.py:709
